TPU v7x, 32 devices: a whole 2x2x4 slice. The times are simulated.
32 devices in a mesh: row: 4 (over x, core), col: 8 (over z, y).
Axes of the slice: x: 2, y: 2, z: 4, core: 2. Of those that a mesh axis runs over, the one named last changes fastest.
Arguments:
- pair: bfloat16 [768, 768, 512], P('row', 'col'), may hold values from -6 to 6
- w_bias: bfloat16 [512, 96], replicated, may hold values from -0.25 to 0.25
- queries: bfloat16 [768, 1536], P('row', 'col'), may hold values from -360 to 360
- keys: bfloat16 [768, 1536], P('col', 'row'), may hold values from -6 to 6
- values: bfloat16 [768, 1536], P('col', 'row'), may hold values from -6 to 6
- d_out: bfloat16 [768, 1536], P('row', 'col'), may hold values from -6 to 6
Outputs:
- d_pair: bfloat16 [768, 768, 512], P('row', 'col')
- d_wbias: float32 [512, 96], replicated
- d_queries: bfloat16 [768, 1536], P('row', 'col')
- d_keys: bfloat16 [768, 1536], P('col', 'row')
- d_values: bfloat16 [768, 1536], P('col', 'row')
All inputs are finite; a program needn't handle non-finite values.
Results may differ from a plain program's by a relative error of at most 0.0095.
Values may be sent and summed in bfloat16 or wider, within the bound.
A program may use at most 128 MiB of HBM per device.

v0:
```python
import jax
import jax.numpy as jnp
from jax import lax
from jax.sharding import PartitionSpec as P

D = 1536
H = 96
P_SIZE = 512
HD = 16


def joined(value, axis, join):
    pieces = jax.tree.map(lambda part: lax.all_gather(part, axis), value)
    head = jax.tree.map(lambda part: part[0], pieces)
    tail = jax.tree.map(lambda part: part[1:], pieces)
    subtotal, _ = lax.scan(lambda subtotal, piece: (join(subtotal, piece), None), head, tail)
    return subtotal


def combine_stats(former, latter):
    joined_max = jnp.maximum(former[0], latter[0])
    scale_former = jnp.exp(former[0] - joined_max)
    scale_latter = jnp.exp(latter[0] - joined_max)
    return (
        joined_max,
        former[1] * scale_former + latter[1] * scale_latter,
        former[2] * scale_former + latter[2] * scale_latter,
    )


def on_device(pair, w_bias, queries, keys, values, d_out):
    row_count = pair.shape[0]
    col_count = pair.shape[1]
    query_full, out_full = (
        lax.all_gather(queries, "col", axis=1, tiled=True),
        lax.all_gather(d_out, "col", axis=1, tiled=True),
    )
    key_full, value_full = (
        lax.all_gather(keys, "row", axis=1, tiled=True),
        lax.all_gather(values, "row", axis=1, tiled=True),
    )
    query_heads = query_full.reshape(row_count, H, HD)
    out_heads = out_full.reshape(row_count, H, HD)
    key_heads = key_full.reshape(col_count, H, HD)
    value_heads = value_full.reshape(col_count, H, HD)
    flat_pair = pair.reshape(row_count * col_count, P_SIZE)
    pair_bias = jnp.dot(flat_pair, w_bias, preferred_element_type=jnp.float32).reshape(
        row_count, col_count, H
    )
    scale = 1.0 / HD**0.5
    scores = jnp.einsum(
        "ihd,jhd->hij", query_heads, key_heads, preferred_element_type=jnp.float32
    ) * scale + pair_bias.transpose(2, 0, 1)
    grad_prob = jnp.einsum(
        "ihd,jhd->hij", out_heads, value_heads, preferred_element_type=jnp.float32
    )
    local_max = jnp.max(scores, axis=-1)
    exp_scores = jnp.exp(scores - local_max[..., None])
    local_stats = (
        local_max,
        jnp.sum(exp_scores, axis=-1),
        jnp.sum(exp_scores * grad_prob, axis=-1),
    )
    row_max, row_total, row_upper = joined(local_stats, "col", combine_stats)
    weights = jnp.exp(scores - row_max[..., None]) / row_total[..., None]
    row_delta = row_upper / row_total
    grad_score = (weights * (grad_prob - row_delta[..., None])).astype(jnp.bfloat16)
    weights_low = weights.astype(jnp.bfloat16)
    score_flat = grad_score.transpose(1, 2, 0).reshape(row_count * col_count, H)
    d_pair = (
        jnp.dot(score_flat, w_bias.T, preferred_element_type=jnp.float32)
        .astype(jnp.bfloat16)
        .reshape(row_count, col_count, P_SIZE)
    )
    weight_term = jnp.dot(flat_pair.T, score_flat, preferred_element_type=jnp.float32)
    d_wbias = lax.psum(weight_term, ("row", "col"))
    query_term = (
        jnp.einsum("hij,jhd->ihd", grad_score, key_heads, preferred_element_type=jnp.float32)
        * scale
    ).reshape(row_count, D)
    key_term = (
        jnp.einsum("hij,ihd->jhd", grad_score, query_heads, preferred_element_type=jnp.float32)
        * scale
    ).reshape(col_count, D)
    value_term = jnp.einsum(
        "hij,ihd->jhd", weights_low, out_heads, preferred_element_type=jnp.float32
    ).reshape(col_count, D)
    query_grad = lax.psum_scatter(query_term, "col", scatter_dimension=1, tiled=True)
    key_grad, value_grad = (
        lax.psum_scatter(key_term, "row", scatter_dimension=1, tiled=True),
        lax.psum_scatter(value_term, "row", scatter_dimension=1, tiled=True),
    )
    return (
        d_pair,
        d_wbias,
        query_grad.astype(jnp.bfloat16),
        key_grad.astype(jnp.bfloat16),
        value_grad.astype(jnp.bfloat16),
    )


def solution(mesh):
    return jax.shard_map(
        on_device,
        mesh=mesh,
        in_specs=(
            P("row", "col", None),
            P(),
            P("row", "col"),
            P("col", "row"),
            P("col", "row"),
            P("row", "col"),
        ),
        out_specs=(P("row", "col", None), P(), P("row", "col"), P("col", "row"), P("col", "row")),
        check_vma=False,
    )
```

profile of v0, /device:TPU:0, one launch (start us, length us, event | category | flops | bytes accessed | tf_op | source)
XLA Modules:
  0.0 433.4 jit_solution(17199849973470065205)
XLA Ops:
  8.9 11.2 %fusion.11 = f32[192,96,96]{2,1,0:T(8,128)} fusion(bf16[192,96,512]{2,1,0:T(8,128)(2,1)} %param.8, bf16[512,96]{0,1:T(8,128)(2,1)S(1)} %copy-done), kind=kOutput, calls=%fused_computation.27 | convolution fusion | flops 1811939328 | bytes 26050560 | tf_op jit(solution)/shard_map/dot_general | solution.py:47
  20.1 12.1 %copy.40 = f32[192,96,96]{0,1,2:T(8,128)} copy(f32[192,96,96]{2,1,0:T(8,128)} %fusion.11) | data formatting | bytes 14155776 | tf_op jit(solution)/shard_map/dot_general | solution.py:47
  32.4 33.9 %all_gather.30 = bf16[192,1536]{0,1:T(8,128)(2,1)S(1)} all-gather(bf16[192,192]{0,1:T(8,128)(2,1)S(1)} %copy.38), channel_id=1, replica_groups=mesh['row'=4,'col'=8] {'col'}, dimensions={1}, use_global_device_ids=true | all-gather | bytes 663552 | tf_op jit(solution)/shard_map/all_gather | solution.py:35
  66.3 5.9 %all_gather.31 = bf16[96,1536]{1,0:T(8,128)(2,1)S(1)} all-gather(bf16[96,384]{1,0:T(8,128)(2,1)S(1)} %copy-done.5), channel_id=1, replica_groups=mesh['row'=4,'col'=8] {'row'}, dimensions={1}, use_global_device_ids=true | all-gather | bytes 368640 | tf_op jit(solution)/shard_map/all_gather | solution.py:39
  72.5 32.3 %all_gather.36 = bf16[192,1536]{0,1:T(8,128)(2,1)S(1)} all-gather(bf16[192,192]{0,1:T(8,128)(2,1)S(1)} %copy.42), channel_id=1, replica_groups=mesh['row'=4,'col'=8] {'col'}, dimensions={1}, use_global_device_ids=true | all-gather | bytes 663552 | tf_op jit(solution)/shard_map/all_gather | solution.py:36
  104.8 5.9 %all_gather.37 = bf16[96,1536]{1,0:T(8,128)(2,1)S(1)} all-gather(bf16[96,384]{1,0:T(8,128)(2,1)S(1)} %copy-done.6), channel_id=1, replica_groups=mesh['row'=4,'col'=8] {'row'}, dimensions={1}, use_global_device_ids=true | all-gather | bytes 368640 | tf_op jit(solution)/shard_map/all_gather | solution.py:40
  110.9 9.2 %fusion.13 = (f32[96,192]{1,0:T(8,128)S(1)}, f32[96,192,96]{1,2,0:T(8,128)S(1)}, f32[96,192,96]{1,2,0:T(8,128)}) fusion(f32[192,96,96]{0,1,2:T(8,128)} %copy.40, bf16[192,96,16]{0,2,1:T(8,128)(2,1)S(1)} %bitcast.92, bf16[96,96,16]{0,2,1:T(8,128)(2,1)S(1)} %bitcast.96), kind=kOutput, calls=%fused_computation.29 | convolution fusion | flops 61913088 | bytes 22192128 | tf_op jit(solution)/shard_map/ihd,jhd->hij/dot_general | solution.py:51
  120.0 5.7 %multiply_reduce_fusion = (f32[96,192]{1,0:T(8,128)S(1)}, f32[96,192]{1,0:T(8,128)S(1)}, f32[96,192,96]{1,2,0:T(8,128)}) fusion(f32[96,192,96]{1,2,0:T(8,128)S(1)} %get-tuple-element.66, f32[96,192]{1,0:T(8,128)S(1)} %get-tuple-element.65, bf16[192,96,16]{0,2,1:T(8,128)(2,1)S(1)} %bitcast.98, bf16[96,96,16]{0,2,1:T(8,128)(2,1)S(1)} %bitcast.103), kind=kOutput, calls=%fused_computation.19 | convolution fusion | flops 63664128 | bytes 15261696 | tf_op jit(solution)/shard_map/ihd,jhd->hij/dot_general | solution.py:54
  126.3 32.1 %all-gather.1 = f32[768,192]{1,0:T(8,128)S(1)} all-gather(f32[96,192]{1,0:T(8,128)S(1)} %get-tuple-element.48), channel_id=3, replica_groups=mesh['row'=4,'col'=8] {'col'}, dimensions={0}, use_global_device_ids=true | all-gather | bytes 663552 | tf_op jit(solution)/shard_map/all_gather | solution.py:13
  159.3 32.3 %all-gather.2 = f32[768,192]{1,0:T(8,128)S(1)} all-gather(f32[96,192]{1,0:T(8,128)S(1)} %get-tuple-element.47), channel_id=4, replica_groups=mesh['row'=4,'col'=8] {'col'}, dimensions={0}, use_global_device_ids=true | all-gather | bytes 663552 | tf_op jit(solution)/shard_map/all_gather | solution.py:13
  192.5 32.0 %all-gather = f32[768,192]{1,0:T(8,128)S(1)} all-gather(f32[96,192]{1,0:T(8,128)S(1)} %get-tuple-element.65), channel_id=2, replica_groups=mesh['row'=4,'col'=8] {'col'}, dimensions={0}, use_global_device_ids=true | all-gather | bytes 663552 | tf_op jit(solution)/shard_map/all_gather | solution.py:13
  224.6 13.8 %while.14 = (s32[]{:T(128)}, f32[96,192]{1,0:T(8,128)S(1)}, f32[96,192]{1,0:T(8,128)S(1)}, f32[96,192]{1,0:T(8,128)S(1)}, f32[7,96,192]{2,1,0:T(8,128)S(1)}, /*i...) while((s32[]{:T(128)}, f32[96,192]{1,0:T(8,128)S(1)}, f32[96,192]{1,0:T(8,128)S(1)}, ...), condition=%wide.region_4.5_spmd, body=%wide.region_3.4_spmd.sunk | while | flops 202754 | bytes 1032285 | solution.py:16
  238.4 6.2 %fusion.9 = f32[96,96,16]{1,2,0:T(8,128)} fusion(bf16[192,96,16]{0,2,1:T(8,128)(2,1)S(1)} %bitcast.99, f32[96,192,96]{1,2,0:T(8,128)} %copy-done.1, f32[96,192]{1,0:T(8,128)S(1)} %get-tuple-element.45, f32[96,192]{1,0:T(8,128)S(1)} %get-tuple-element.44), kind=kOutput, calls=%fused_computation.22 | convolution fusion | flops 61931520 | bytes 8404992 | tf_op jit(solution)/shard_map/hij,ihd->jhd/dot_general | solution.py:85
  244.6 2.2 copy.51
  247.1 8.0 %multiply_convert_fusion = bf16[96,192,96]{1,2,0:T(8,128)(2,1)S(1)} fusion(f32[96,192,96]{1,2,0:T(8,128)} %get-tuple-element.68, f32[96,192]{1,0:T(8,128)S(1)} %div.21, f32[96,192]{1,0:T(8,128)S(1)} %get-tuple-element.45, f32[96,192,96]{1,2,0:T(8,128)} %copy-done.1, f32[96,192]{1,0:T(8,128)S(1)} %get-tuple-element.44), kind=kLoop, calls=%fused_computation.17 | loop fusion | flops 8847360 | bytes 17915904 | tf_op jit(solution)/shard_map/convert_element_type | solution.py:67
  259.8 4.2 convolution_multiply_fusion
  264.1 13.0 %fusion.4 = bf16[192,96,96]{0,1,2:T(8,128)(2,1)} fusion(f32[96,192,96]{1,2,0:T(8,128)} %get-tuple-element.68, f32[192,96,96]{0,1,2:T(8,128)} %copy.40, f32[96,192,96]{1,2,0:T(8,128)} %get-tuple-element.67, f32[192,96]{0,1:T(8,128)S(1)} %bitcast.104, f32[192,96]{0,1:T(8,128)S(1)} %bitcast.91, f32[192,96]{0,1:T(8,128)S(1)} %bitcast.90), kind=kLoop, calls=%fused_computation.11 | loop fusion | flops 12386304 | bytes 24993792 | tf_op jit(solution)/shard_map/convert_element_type | solution.py:67
  277.1 7.5 %copy.45 = bf16[192,96,96]{1,2,0:T(8,128)(2,1)} copy(bf16[192,96,96]{0,1,2:T(8,128)(2,1)} %fusion.4) | data formatting | bytes 7077888 | tf_op jit(solution)/shard_map/convert_element_type | solution.py:67
  284.7 11.8 %convolution_bitcast_fusion = f32[512,96]{0,1:T(8,128)} fusion(bf16[192,96,96]{1,2,0:T(8,128)(2,1)} %copy.45, bf16[192,96,512]{2,1,0:T(8,128)(2,1)} %param.8), kind=kOutput, calls=%fused_computation.26 | convolution fusion | flops 1811939328 | bytes 22609920 | tf_op jit(solution)/shard_map/dot_general | solution.py:75
  296.4 6.7 %copy.44 = bf16[192,96,96]{1,0,2:T(8,128)(2,1)} copy(bf16[192,96,96]{0,1,2:T(8,128)(2,1)} %fusion.4) | data formatting | bytes 7077888 | tf_op jit(solution)/shard_map/convert_element_type | solution.py:67
  303.2 9.2 %reshape.49 = bf16[18432,96]{0,1:T(8,128)(2,1)} reshape(bf16[192,96,96]{1,0,2:T(8,128)(2,1)} %copy.44) | data formatting | bytes 7077888 | tf_op jit(solution)/shard_map/reshape | solution.py:69
  312.4 11.5 %convolution_convert_fusion = bf16[18432,512]{1,0:T(8,128)(2,1)} fusion(bf16[18432,96]{0,1:T(8,128)(2,1)} %reshape.49, bf16[512,96]{0,1:T(8,128)(2,1)S(1)} %copy-done), kind=kOutput, calls=%fused_computation.8 | convolution fusion | flops 1821376512 | bytes 22511616 | tf_op jit(solution)/shard_map/dot_general | solution.py:71
  327.0 36.4 %reduce-scatter.10.cloned.1.call-done = f32[192,192]{1,0:T(8,128)} async-done(((f32[1536,192]{1,0:T(8,128)}), f32[192,192]{1,0:T(8,128)}) %reduce-scatter.10.cloned.1.call-update) | async-done | bytes 147472
  365.1 59.6 %all-reduce.2.cloned.1.call-done = f32[512,96]{0,1:T(8,128)} async-done(((f32[512,96]{0,1:T(8,128)}), f32[512,96]{0,1:T(8,128)}) %all-reduce.2.cloned.1.call-update) | async-done | bytes 196624 | tf_op jit(solution)/shard_map/psum | solution.py:76
  (62 shorter events, 29.1 us)
Async XLA Ops:
  8.0 0.9 copy-start
  8.0 315.9 %reduce-scatter.8.cloned.1.call-start = ((), (), s32[]{:S(2)}) async-start(), calls=%async_computation.5 | async-start | bytes 737280 | tf_op jit(solution)/shard_map/reduce_scatter | solution.py:91
  20.1 12.2 %copy-start.3 = (bf16[192,192]{1,0:T(8,128)(2,1)S(1)}, bf16[192,192]{1,0:T(8,128)(2,1)}, u32[]{:S(2)}) copy-start(bf16[192,192]{1,0:T(8,128)(2,1)} %param.10) | copy-start | bytes 221188
  20.1 46.2 %copy-start.5 = (bf16[96,384]{1,0:T(8,128)(2,1)S(1)}, bf16[96,384]{1,0:T(8,128)(2,1)}, u32[]{:S(2)}) copy-start(bf16[96,384]{1,0:T(8,128)(2,1)} %param.11) | copy-start | bytes 221188
  20.1 52.3 %copy-start.4 = (bf16[192,192]{1,0:T(8,128)(2,1)S(1)}, bf16[192,192]{1,0:T(8,128)(2,1)}, u32[]{:S(2)}) copy-start(bf16[192,192]{1,0:T(8,128)(2,1)} %param.13) | copy-start | bytes 221188
  20.1 84.7 %copy-start.6 = (bf16[96,384]{1,0:T(8,128)(2,1)S(1)}, bf16[96,384]{1,0:T(8,128)(2,1)}, u32[]{:S(2)}) copy-start(bf16[96,384]{1,0:T(8,128)(2,1)} %param.12) | copy-start | bytes 221188
  120.0 6.3 %copy-start.1 = (f32[96,192,96]{1,2,0:T(8,128)}, f32[96,192,96]{1,2,0:T(8,128)S(1)}, u32[]{:S(2)}) copy-start(f32[96,192,96]{1,2,0:T(8,128)S(1)} %get-tuple-element.66) | copy-start | bytes 21233668
  246.9 78.6 %reduce-scatter.6.cloned.1.call-start = ((), (), s32[]{:S(2)}) async-start(), calls=%async_computation.4 | async-start | bytes 737280 | tf_op jit(solution)/shard_map/reduce_scatter | solution.py:90
  255.1 2.2 copy-start.2
  259.8 103.7 %reduce-scatter.10.cloned.1.call-start = ((), (), s32[]{:S(2)}) async-start(), calls=%async_computation.6 | async-start | bytes 1769472
  264.1 160.6 %all-reduce.2.cloned.1.call-start = ((), (), s32[]{:S(2)}) async-start(), calls=%async_computation.3 | async-start | bytes 393216 | tf_op jit(solution)/shard_map/psum | solution.py:76
Sparse Core Ops, SparseCore 0:
  247.0 22.7 reduce-scatter.7
  272.3 22.0 reduce-scatter.5
  297.8 65.6 reduce-scatter.9
Sparse Core Ops, SparseCore 1:
  296.5 128.1 all-reduce.1
where the time goes:
time: 435 us; the launch traced here: 433 us
  blocking collectives  174 us (40%)
  waiting for transfers between devices  96 us (22%)
  matrix products  61.1 us (14%)
  local copies, waits for them, and re-layouts  48.5 us (11%)
  other arithmetic  37.7 us (9%)
  between operations  15.3 us (4%)
    all_gather x3, blocking collectives, joined(): pieces = jax.tree.map(lambda part: lax.all_gather(part, axis), value)  96.4 us
    psum x1, waiting for transfers between devices, on_device(): d_wbias = lax.psum(weight_term, ('row', 'col'))  59.6 us
    unnamed x5, waiting for transfers between devices  36.5 us
    all_gather x1, blocking collectives, on_device(): lax.all_gather(queries, 'col', axis=1, tiled=True)  33.9 us
    all_gather x1, blocking collectives, on_device(): lax.all_gather(d_out, 'col', axis=1, tiled=True)  32.3 us
    convert_element_type x2, other arithmetic, on_device(): (weights * (grad_prob - row_delta[..., None])).astype(jnp.bfloat16)  21 us
    convert_element_type x2, local copies, waits for them, and re-layouts, on_device(): (weights * (grad_prob - row_delta[..., None])).astype(jnp.bfloat16)  14.3 us
    dot_general x1, local copies, waits for them, and re-layouts, on_device(): jnp.dot(flat_pair, w_bias, preferred_element_type=jnp.float32)  12.1 us
  transfers between devices with their start and end apart: 4, of which 2 were waited for; matrix products, arithmetic and copies ran while one was open for 18% of the time, Pallas kernels for 0%

commit v1 on v0

v1 whole, which is shorter than its diff:
```python
import functools

import jax
import jax.numpy as jnp
from jax import lax
from jax.experimental import pallas as pl
from jax.experimental.pallas import tpu as pltpu
from jax.sharding import PartitionSpec as P

H = 96
HD = 16
SCALE = 1.0 / HD**0.5
MESH = pl.DeviceIdType.MESH
VMEM = pltpu.VMEM
DMA = pltpu.SemaphoreType.DMA


def remote(src, dst, send, recv, row, col):
    return pltpu.make_async_remote_copy(
        src_ref=src, dst_ref=dst, send_sem=send, recv_sem=recv,
        device_id=(row, col), device_id_type=MESH,
    )


def greet(nrow, ncol, row, col):
    barrier = pltpu.get_barrier_semaphore()
    for k in range(1, ncol):
        pl.semaphore_signal(
            barrier, inc=1, device_id=(row, lax.rem(col + k, ncol)), device_id_type=MESH
        )
    for k in range(1, nrow):
        pl.semaphore_signal(
            barrier, inc=1, device_id=(lax.rem(row + k, nrow), col), device_id_type=MESH
        )
    pl.semaphore_wait(barrier, ncol + nrow - 2)


def gather_kernel(nrow, ncol, qd, kv, qd_all, kv_all, qs, qr, fs, fr, ks, kr):
    row, col = lax.axis_index("row"), lax.axis_index("col")
    inner = 2 if ncol % 2 == 0 else 1
    outer = ncol // inner
    a, b = col // inner, lax.rem(col, inner)
    greet(nrow, ncol, row, col)
    sends = []
    for k in range(1, outer):
        to = lax.rem(a + k, outer) * inner + b
        sends.append(remote(qd, qd_all.at[col], qs.at[k], qr.at[k], row, to))
    if inner == 2:
        sends.append(remote(qd, qd_all.at[col], fs.at[0], fr.at[0], row, a * inner + 1 - b))
    for k in range(1, nrow):
        sends.append(remote(kv, kv_all.at[row], ks.at[k], kr.at[k], lax.rem(row + k, nrow), col))
    for copy in sends:
        copy.start()
    qd_all[col] = qd[...]
    kv_all[row] = kv[...]
    for k in range(1, outer):
        src = lax.rem(a + outer - k, outer) * inner + b
        remote(qd, qd_all.at[src], qs.at[k], qr.at[k], row, col).wait_recv()
        if inner == 2:
            copy = remote(
                qd_all.at[src], qd_all.at[src], fs.at[k], fr.at[k], row, a * inner + 1 - b
            )
            copy.start()
            sends.append(copy)
    if inner == 2:
        for k in range(outer):
            src = lax.rem(a + outer - k, outer) * inner + 1 - b
            remote(qd, qd_all.at[src], fs.at[k], fr.at[k], row, col).wait_recv()
    for k in range(1, nrow):
        src = lax.rem(row + nrow - k, nrow)
        remote(kv, kv_all.at[src], ks.at[k], kr.at[k], row, col).wait_recv()
    for copy in sends:
        copy.wait_send()


def gather(nrow, ncol, qd, kv):
    return pl.pallas_call(
        functools.partial(gather_kernel, nrow, ncol),
        out_shape=(
            jax.ShapeDtypeStruct((ncol,) + qd.shape, qd.dtype),
            jax.ShapeDtypeStruct((nrow,) + kv.shape, kv.dtype),
        ),
        in_specs=[pl.BlockSpec(memory_space=VMEM)] * 2,
        out_specs=[pl.BlockSpec(memory_space=VMEM)] * 2,
        scratch_shapes=[DMA((ncol,))] * 4 + [DMA((nrow,))] * 2,
        compiler_params=pltpu.CompilerParams(collective_id=0, has_side_effects=True),
    )(qd, kv)


def stats_kernel(ncol, st, out, got, back, s1, r1, s2, r2):
    row, col = lax.axis_index("row"), lax.axis_index("col")
    barrier = pltpu.get_barrier_semaphore()
    for k in range(1, ncol):
        pl.semaphore_signal(
            barrier, inc=1, device_id=(row, lax.rem(col + k, ncol)), device_id_type=MESH
        )
    pl.semaphore_wait(barrier, ncol - 1)
    sends = []
    for k in range(1, ncol):
        to = lax.rem(col + k, ncol)
        copy = remote(st.at[to], got.at[k], s1.at[k], r1.at[k], row, to)
        copy.start()
        sends.append(copy)
    got[0] = st[col]
    for k in range(1, ncol):
        remote(st.at[k], got.at[k], s1.at[k], r1.at[k], row, col).wait_recv()
    top = got[0, 0]
    for k in range(1, ncol):
        top = jnp.maximum(top, got[k, 0])
    total = jnp.zeros_like(top)
    upper = jnp.zeros_like(top)
    scales = []
    for k in range(ncol):
        scale = jnp.exp(got[k, 0] - top)
        scales.append(scale)
        total += got[k, 1] * scale
        upper += got[k, 2] * scale
    delta = upper / total
    for k in range(ncol):
        back[k, 0] = scales[k] / total
        back[k, 1] = delta
    for k in range(1, ncol):
        to = lax.rem(col + ncol - k, ncol)
        copy = remote(back.at[k], out.at[col], s2.at[k], r2.at[k], row, to)
        copy.start()
        sends.append(copy)
    out[col] = back[0]
    for k in range(1, ncol):
        src = lax.rem(col + k, ncol)
        remote(back.at[k], out.at[src], s2.at[k], r2.at[k], row, col).wait_recv()
    for copy in sends:
        copy.wait_send()


def stats(ncol, st):
    part = st.shape[2:]
    return pl.pallas_call(
        functools.partial(stats_kernel, ncol),
        out_shape=jax.ShapeDtypeStruct((ncol, 2) + part, jnp.float32),
        in_specs=[pl.BlockSpec(memory_space=VMEM)],
        out_specs=pl.BlockSpec(memory_space=VMEM),
        scratch_shapes=[
            VMEM((ncol, 3) + part, jnp.float32),
            VMEM((ncol, 2) + part, jnp.float32),
        ]
        + [DMA((ncol,))] * 4,
        compiler_params=pltpu.CompilerParams(collective_id=1, has_side_effects=True),
    )(st)


def reduce_kernel(
    nrow, ncol, wb, dq, dkv, wb_out, q_out, kv_out,
    w1, w1sum, w2, w2sum, qgot, kgot, ws1, wr1, ws2, wr2, ws3, wr3, ws4, wr4, qs, qr, ks, kr,
):
    row, col = lax.axis_index("row"), lax.axis_index("col")
    greet(nrow, ncol, row, col)
    sends = []

    def go(copy):
        copy.start()
        sends.append(copy)

    for k in range(1, nrow):
        to = lax.rem(row + k, nrow)
        go(remote(wb.at[to], w1.at[k], ws1.at[k], wr1.at[k], to, col))
    for k in range(1, ncol):
        to = lax.rem(col + k, ncol)
        go(remote(dq.at[to], qgot.at[k], qs.at[k], qr.at[k], row, to))
    for k in range(1, nrow):
        to = lax.rem(row + k, nrow)
        go(remote(dkv.at[to], kgot.at[k], ks.at[k], kr.at[k], to, col))
    total = wb[row]
    for k in range(1, nrow):
        remote(wb.at[0], w1.at[k], ws1.at[k], wr1.at[k], row, col).wait_recv()
        total += w1[k]
    w1sum[...] = total
    for k in range(1, ncol):
        to = lax.rem(col + k, ncol)
        go(remote(w1sum.at[to], w2.at[k], ws2.at[k], wr2.at[k], row, to))
    part = w1sum[col]
    for k in range(1, ncol):
        remote(w1sum.at[0], w2.at[k], ws2.at[k], wr2.at[k], row, col).wait_recv()
        part += w2[k]
    w2sum[...] = part
    for k in range(1, ncol):
        to = lax.rem(col + k, ncol)
        go(remote(w2sum, wb_out.at[row, col], ws3.at[k], wr3.at[k], row, to))
    wb_out[row, col] = part
    for k in range(1, ncol):
        src = lax.rem(col + ncol - k, ncol)
        remote(w2sum, wb_out.at[row, src], ws3.at[k], wr3.at[k], row, col).wait_recv()
    for k in range(1, nrow):
        to = lax.rem(row + k, nrow)
        go(remote(wb_out.at[row], wb_out.at[row], ws4.at[k], wr4.at[k], to, col))
    grad = dkv[row].astype(jnp.float32)
    for k in range(1, nrow):
        remote(dkv.at[0], kgot.at[k], ks.at[k], kr.at[k], row, col).wait_recv()
        grad += kgot[k].astype(jnp.float32)
    kv_out[...] = grad.astype(kv_out.dtype)
    grad = dq[col].astype(jnp.float32)
    for k in range(1, ncol):
        remote(dq.at[0], qgot.at[k], qs.at[k], qr.at[k], row, col).wait_recv()
        grad += qgot[k].astype(jnp.float32)
    q_out[...] = grad.astype(q_out.dtype)
    for k in range(1, nrow):
        src = lax.rem(row + nrow - k, nrow)
        remote(wb_out.at[src], wb_out.at[src], ws4.at[k], wr4.at[k], row, col).wait_recv()
    for copy in sends:
        copy.wait_send()


def reduce_all(nrow, ncol, wb, dq, dkv):
    chunk = wb.shape[2:]
    return pl.pallas_call(
        functools.partial(reduce_kernel, nrow, ncol),
        out_shape=(
            jax.ShapeDtypeStruct(wb.shape, jnp.float32),
            jax.ShapeDtypeStruct(dq.shape[1:], jnp.bfloat16),
            jax.ShapeDtypeStruct(dkv.shape[1:], jnp.bfloat16),
        ),
        in_specs=[pl.BlockSpec(memory_space=VMEM)] * 3,
        out_specs=[pl.BlockSpec(memory_space=VMEM)] * 3,
        scratch_shapes=[
            VMEM(wb.shape, jnp.float32),
            VMEM((ncol,) + chunk, jnp.float32),
            VMEM((ncol,) + chunk, jnp.float32),
            VMEM(chunk, jnp.float32),
            VMEM(dq.shape, dq.dtype),
            VMEM(dkv.shape, dkv.dtype),
            DMA((nrow,)), DMA((nrow,)), DMA((ncol,)), DMA((ncol,)),
            DMA((ncol,)), DMA((ncol,)), DMA((nrow,)), DMA((nrow,)),
            DMA((ncol,)), DMA((ncol,)), DMA((nrow,)), DMA((nrow,)),
        ],
        compiler_params=pltpu.CompilerParams(collective_id=2, has_side_effects=True),
    )(wb, dq, dkv)


def on_device(nrow, ncol, pair, w_bias, queries, keys, values, d_out):
    R, C, width = pair.shape
    dcol, drow = queries.shape[1], keys.shape[1]
    qd_all, kv_all = gather(
        nrow, ncol,
        jnp.concatenate([queries, d_out], axis=1),
        jnp.concatenate([keys, values], axis=1),
    )
    query_heads = qd_all[:, :, :dcol].transpose(1, 0, 2).reshape(R, H, HD)
    out_heads = qd_all[:, :, dcol:].transpose(1, 0, 2).reshape(R, H, HD)
    key_heads = kv_all[:, :, :drow].transpose(1, 0, 2).reshape(C, H, HD)
    value_heads = kv_all[:, :, drow:].transpose(1, 0, 2).reshape(C, H, HD)
    flat_pair = pair.reshape(R * C, width)
    pair_bias = jnp.dot(flat_pair, w_bias, preferred_element_type=jnp.float32).reshape(R, C, H)
    scores = jnp.einsum(
        "ihd,jhd->hij", query_heads, key_heads, preferred_element_type=jnp.float32
    ) * SCALE + pair_bias.transpose(2, 0, 1)
    grad_prob = jnp.einsum(
        "ihd,jhd->hij", out_heads, value_heads, preferred_element_type=jnp.float32
    )
    local_max = jnp.max(scores, axis=-1)
    exp_scores = jnp.exp(scores - local_max[..., None])
    st = jnp.stack(
        [local_max, jnp.sum(exp_scores, axis=-1), jnp.sum(exp_scores * grad_prob, axis=-1)]
    )
    st = st.reshape(3, ncol, H // ncol, R).transpose(1, 0, 2, 3)
    back = stats(ncol, st).transpose(1, 0, 2, 3).reshape(2, H, R)
    weights = exp_scores * back[0][..., None]
    grad_score = (weights * (grad_prob - back[1][..., None])).astype(jnp.bfloat16)
    weights_low = weights.astype(jnp.bfloat16)
    score_flat = grad_score.transpose(1, 2, 0).reshape(R * C, H)
    d_pair = (
        jnp.dot(score_flat, w_bias.T, preferred_element_type=jnp.float32)
        .astype(jnp.bfloat16)
        .reshape(R, C, width)
    )
    weight_term = jnp.dot(score_flat.T, flat_pair, preferred_element_type=jnp.float32)
    query_term = jnp.einsum(
        "hij,jhd->ihd", grad_score, key_heads, preferred_element_type=jnp.float32
    ) * SCALE
    key_term = jnp.einsum(
        "hij,ihd->jhd", grad_score, query_heads, preferred_element_type=jnp.float32
    ) * SCALE
    value_term = jnp.einsum(
        "hij,ihd->jhd", weights_low, out_heads, preferred_element_type=jnp.float32
    )
    dq = query_term.astype(jnp.bfloat16).reshape(R, ncol, dcol).transpose(1, 0, 2)
    dk = key_term.astype(jnp.bfloat16).reshape(C, nrow, drow).transpose(1, 0, 2)
    dv = value_term.astype(jnp.bfloat16).reshape(C, nrow, drow).transpose(1, 0, 2)
    wb = weight_term.reshape(ncol, H // ncol, nrow, width // nrow).transpose(2, 0, 1, 3)
    wb, q_grad, kv_grad = reduce_all(nrow, ncol, wb, dq, jnp.concatenate([dk, dv], axis=2))
    d_wbias = wb.transpose(0, 3, 1, 2).reshape(width, H)
    return d_pair, d_wbias, q_grad, kv_grad[:, :drow], kv_grad[:, drow:]


def solution(mesh):
    return jax.shard_map(
        functools.partial(on_device, mesh.shape["row"], mesh.shape["col"]),
        mesh=mesh,
        in_specs=(
            P("row", "col", None),
            P(),
            P("row", "col"),
            P("col", "row"),
            P("col", "row"),
            P("row", "col"),
        ),
        out_specs=(P("row", "col", None), P(), P("row", "col"), P("col", "row"), P("col", "row")),
        check_vma=False,
    )
```

time: 435 us -> 251 us (0.58)
  blocking collectives: 174 us -> 0 us
  waiting for transfers between devices: 96 us -> 0 us
  Pallas kernels: 0 us -> 83.5 us
  local copies, waits for them, and re-layouts: 48.5 us -> 68.3 us
  between operations: 15.3 us -> 0.77 us
  other arithmetic: 37.7 us -> 29.7 us
  matrix products: 61.1 us -> 66.8 us
    all_gather x7 -> x0, blocking collectives: 174 us -> none  [the longest x3 96.4 us: joined(): pieces = jax.tree.map(lambda part: lax.all_gather(part, axis), value)]
    pallas_call x0 -> x3, Pallas kernels: none -> 83.5 us  [the longest x1 30.6 us: reduce_all(): pl.pallas_call(functools.partial(reduce_kernel, nrow, ncol), out_shape=(j...]
    psum x1 -> x0, waiting for transfers between devices: 59.6 us -> none  [on_device(): d_wbias = lax.psum(weight_term, ('row', 'col'))]
    unnamed x5 -> x0, waiting for transfers between devices: 36.5 us -> none
    dot_general x0 -> x2, local copies, waits for them, and re-layouts: none -> 29.6 us  [on_device(): jnp.dot(score_flat.T, flat_pair, preferred_element_type=jnp.float32)]
    add x14 -> x0, other arithmetic: 13.6 us -> none  [the longest x7 6.82 us: combine_stats(): former[2] * scale_former + latter[2] * scale_latter]
    convert_element_type x2 -> x1, local copies, waits for them, and re-layouts: 14.3 us -> 6.75 us  [on_device(): (weights * (grad_prob - back[1][..., None])).astype(jnp.bfloat16)]
    unnamed x18 -> x6, local copies, waits for them, and re-layouts: 7.11 us -> 1.34 us
  transfers between devices with their start and end apart: 4 -> 0, of which waited for: 2 -> 0; matrix products, arithmetic and copies ran while one was open for 18% -> 0% of each run, Pallas kernels for 0% -> 0%
where the time goes in v1:
time: 251 us; the launch traced here: 249 us
  Pallas kernels  83.5 us (33%)
  local copies, waits for them, and re-layouts  68.3 us (27%)
  matrix products  66.8 us (27%)
  other arithmetic  29.7 us (12%)
    pallas_call x1, Pallas kernels, reduce_all(): pl.pallas_call(functools.partial(reduce_kernel, nrow, ncol), out_shape=(j...  30.6 us
    dot_general x2, local copies, waits for them, and re-layouts, on_device(): jnp.dot(score_flat.T, flat_pair, preferred_element_type=jnp.float32)  29.6 us
    pallas_call x1, Pallas kernels, gather(): pl.pallas_call(functools.partial(gather_kernel, nrow, ncol), out_shape=(j...  26.8 us
    pallas_call x1, Pallas kernels, stats(): pl.pallas_call(functools.partial(stats_kernel, ncol), out_shape=jax.Shape...  26.2 us
    convert_element_type x2, other arithmetic, on_device(): (weights * (grad_prob - back[1][..., None])).astype(jnp.bfloat16)  24.7 us
    dot_general x1, matrix products, on_device(): jnp.einsum('ihd,jhd->hij', query_heads, key_heads, preferred_element_type...  12.2 us
    dot_general x1, matrix products, on_device(): jnp.dot(score_flat.T, flat_pair, preferred_element_type=jnp.float32)  12.2 us
    dot_general x1, local copies, waits for them, and re-layouts, on_device(): jnp.dot(flat_pair, w_bias, preferred_element_type=jnp.float32)  12.1 us

profile of v1, /device:TPU:0, one launch (start us, length us, event | category | flops | bytes accessed | tf_op | source)
XLA Modules:
  0.0 249.1 jit_solution(3396805568949858461)
XLA Ops:
  0.6 1.7 pad_maximum_fusion.1.qd
  2.4 1.6 pad_maximum_fusion.2.kv
  4.0 26.8 %shard_map.101 = (bf16[8,192,384]{2,1,0:T(8,128)(2,1)}, bf16[4,96,768]{2,1,0:T(8,128)(2,1)}) custom-call(bf16[192,384]{1,0:T(8,128)(2,1)} %pad_maximum_fusion.1.qd, bf16[96,768]{1,0:T(8,128)(2,1)} %pad_maximum_fusion.2.kv), custom_call_target="tpu_custom_call" | custom-call | tf_op jit(solution)/shard_map/pallas_call | solution.py:77
  30.8 1.8 slice_bitcast_fusion.1
  32.9 1.1 slice_bitcast_fusion.3
  34.2 11.2 %fusion.11 = f32[192,96,96]{2,1,0:T(8,128)} fusion(bf16[192,96,512]{2,1,0:T(8,128)(2,1)} %param.6, bf16[512,96]{0,1:T(8,128)(2,1)S(1)} %copy-done), kind=kOutput, calls=%fused_computation.31 | convolution fusion | flops 1811939328 | bytes 26050560 | tf_op jit(solution)/shard_map/dot_general | solution.py:251
  45.4 12.1 %copy.20 = f32[192,96,96]{0,1,2:T(8,128)} copy(f32[192,96,96]{2,1,0:T(8,128)} %fusion.11) | data formatting | bytes 14155776 | tf_op jit(solution)/shard_map/dot_general | solution.py:251
  57.5 12.2 %fusion.13 = (f32[96,192]{1,0:T(8,128)S(1)}, f32[96,192,96]{1,2,0:T(8,128)}, f32[96,192,96]{1,2,0:T(8,128)}) fusion(f32[192,96,96]{0,1,2:T(8,128)} %copy.20, bf16[192,96,16]{0,2,1:T(8,128)(2,1)S(1)} %bitcast.101, bf16[96,96,16]{0,2,1:T(8,128)(2,1)S(1)} %bitcast.103), kind=kOutput, calls=%fused_computation.33 | convolution fusion | flops 61913088 | bytes 22192128 | tf_op jit(solution)/shard_map/ihd,jhd->hij/dot_general | solution.py:252
  70.3 7.6 %fusion.5 = (f32[96,192]{1,0:T(8,128)S(1)}, f32[96,192]{1,0:T(8,128)S(1)}, f32[96,192,96]{1,2,0:T(8,128)}) fusion(f32[96,192,96]{1,2,0:T(8,128)} %get-tuple-element.18, f32[96,192]{1,0:T(8,128)S(1)} %get-tuple-element.17, bf16[192,96,16]{0,2,1:T(8,128)(2,1)S(1)} %bitcast.99, bf16[96,96,16]{0,2,1:T(8,128)(2,1)S(1)} %bitcast.110), kind=kOutput, calls=%fused_computation.13 | convolution fusion | flops 63664128 | bytes 15261696 | tf_op jit(solution)/shard_map/ihd,jhd->hij/dot_general | solution.py:255
  78.7 26.2 %shard_map.102 = f32[8,2,12,192]{3,2,1,0:T(8,128)} custom-call(f32[8,3,12,192]{3,2,1,0:T(8,128)} %maximum_bitcast_fusion.st), custom_call_target="tpu_custom_call" | custom-call | tf_op jit(solution)/shard_map/pallas_call | solution.py:137
  105.9 11.8 %multiply_convert_fusion = bf16[96,192,96]{1,2,0:T(8,128)(2,1)} fusion(f32[96,192,96]{1,2,0:T(8,128)} %get-tuple-element.28, f32[96,192,96]{1,2,0:T(8,128)} %get-tuple-element.18, f32[96,192]{1,0:T(8,128)S(1)} %sub.37, f32[96,192]{1,0:T(8,128)S(1)} %mul.54, f32[96,192]{1,0:T(8,128)S(1)} %get-tuple-element.17), kind=kLoop, calls=%fused_computation.9 | loop fusion | flops 8847360 | bytes 17915904 | tf_op jit(solution)/shard_map/convert_element_type | solution.py:266
  117.8 3.7 %fusion.10 = bf16[96,16,96]{2,1,0:T(8,128)(2,1)S(1)} fusion(bf16[192,96,16]{0,2,1:T(8,128)(2,1)S(1)} %bitcast.102, bf16[96,192,96]{1,2,0:T(8,128)(2,1)} %multiply_convert_fusion), kind=kOutput, calls=%fused_computation.20 | convolution fusion | flops 56918016 | bytes 4423680 | tf_op jit(solution)/shard_map/hij,ihd->jhd/dot_general | solution.py:278
  121.6 5.2 %fusion.9 = bf16[96,16,96]{2,1,0:T(8,128)(2,1)S(1)} fusion(bf16[192,96,16]{0,2,1:T(8,128)(2,1)S(1)} %bitcast.100, f32[96,192,96]{1,2,0:T(8,128)} %get-tuple-element.18, f32[96,192]{1,0:T(8,128)S(1)} %mul.54, f32[96,192]{1,0:T(8,128)S(1)} %get-tuple-element.17), kind=kOutput, calls=%fused_computation.19 | convolution fusion | flops 62078976 | bytes 8110080 | tf_op jit(solution)/shard_map/hij,ihd->jhd/dot_general | solution.py:281
  128.0 3.1 %multiply_convert_fusion.3 = bf16[96,16,192]{2,1,0:T(8,128)(2,1)S(1)} fusion(bf16[96,96,16]{0,2,1:T(8,128)(2,1)S(1)} %bitcast.104, bf16[96,192,96]{1,2,0:T(8,128)(2,1)} %multiply_convert_fusion), kind=kOutput, calls=%fused_computation.17 | convolution fusion | flops 57212928 | bytes 4423680 | tf_op jit(solution)/shard_map/hij,jhd->ihd/dot_general | solution.py:275
  131.0 1.2 copy.31
  132.3 12.9 %fusion.1 = bf16[192,96,96]{0,1,2:T(8,128)(2,1)} fusion(f32[96,192,96]{1,2,0:T(8,128)} %get-tuple-element.28, f32[192,96,96]{0,1,2:T(8,128)} %copy.20, f32[96,192,96]{1,2,0:T(8,128)} %get-tuple-element.27, f32[192,96]{0,1:T(8,128)S(1)} %bitcast.115, f32[192,96]{0,1:T(8,128)S(1)} %bitcast.108, f32[192,96]{0,1:T(8,128)S(1)} %bitcast.105), kind=kLoop, calls=%fused_computation.3 | loop fusion | flops 12386304 | bytes 24993792 | tf_op jit(solution)/shard_map/convert_element_type | solution.py:266
  145.1 6.7 %copy.27 = bf16[192,96,96]{1,0,2:T(8,128)(2,1)} copy(bf16[192,96,96]{0,1,2:T(8,128)(2,1)} %fusion.1) | data formatting | bytes 7077888 | tf_op jit(solution)/shard_map/convert_element_type | solution.py:266
  151.9 9.2 %reshape.68 = bf16[18432,96]{0,1:T(8,128)(2,1)} reshape(bf16[192,96,96]{1,0,2:T(8,128)(2,1)} %copy.27) | data formatting | bytes 7077888 | tf_op jit(solution)/shard_map/reshape | solution.py:268
  161.1 5.0 %reshape.76 = bf16[8,12,18432,1]{2,1,0,3:T(8,128)(2,1)} reshape(bf16[96,18432]{1,0:T(8,128)(2,1)} %bitcast.96) | data formatting | bytes 7077888 | tf_op jit(solution)/shard_map/dot_general | solution.py:274
  166.1 24.6 %copy.28 = bf16[512,18432]{1,0:T(8,128)(2,1)} copy(bf16[512,18432]{0,1:T(8,128)(2,1)} %bitcast.95) | data formatting | bytes 37748736 | tf_op jit(solution)/shard_map/dot_general | solution.py:274
  190.6 12.2 %convolution_bitcast_fusion.wb = f32[4,8,12,128]{3,2,1,0:T(8,128)} fusion(bf16[8,12,18432,1]{2,1,0,3:T(8,128)(2,1)} %reshape.76, bf16[4,128,18432,1]{2,1,3,0:T(8,128)(2,1)} %bitcast.98), kind=kOutput, calls=%fused_computation.21 | convolution fusion | flops 1811939328 | bytes 22609920 | tf_op jit(solution)/shard_map/dot_general | solution.py:274
  202.9 30.6 %shard_map.103 = (f32[4,8,12,128]{3,2,1,0:T(8,128)}, bf16[192,192]{1,0:T(8,128)(2,1)}, bf16[96,768]{1,0:T(8,128)(2,1)}) custom-call(f32[4,8,12,128]{3,2,1,0:T(8,128)} %convolution_bitcast_fusion.wb, bf16[8,192,192]{2,1,0:T(8,128)(2,1)} %bitcast.106, bf16[4,96,768]{2,1,0:T(8,128)(2,1)} %pad_maximum_fusion.dkv), custom_call_target="tpu_custom_call" | custom-call | tf_op jit(solution)/shard_map/pallas_call | solution.py:214
  235.3 1.6 fusion.15
  236.9 11.5 %convolution_convert_fusion = bf16[18432,512]{1,0:T(8,128)(2,1)} fusion(bf16[18432,96]{0,1:T(8,128)(2,1)} %reshape.68, bf16[512,96]{0,1:T(8,128)(2,1)S(1)} %copy-done), kind=kOutput, calls=%fused_computation | convolution fusion | flops 1821376512 | bytes 22511616 | tf_op jit(solution)/shard_map/dot_general | solution.py:270
  (21 shorter events, 6.7 us)
Async XLA Ops:
  0.6 33.6 %copy-start = (bf16[512,96]{0,1:T(8,128)(2,1)S(1)}, bf16[512,96]{0,1:T(8,128)(2,1)}, u32[]{:S(2)}) copy-start(bf16[512,96]{0,1:T(8,128)(2,1)} %param.7) | copy-start | bytes 294916
  236.9 11.6 %copy-start.1 = (bf16[192,192]{1,0:T(8,128)(2,1)S(1)}, bf16[192,192]{1,0:T(8,128)(2,1)}, u32[]{:S(2)}) copy-start(bf16[192,192]{1,0:T(8,128)(2,1)} %get-tuple-element.36) | copy-start | bytes 221188

commit v2 on v1

--- a/solution.py
+++ b/solution.py
@@ -235,6 +235,77 @@
     )(wb, dq, dkv)
 
 
+def bias_kernel(wt, pair, out):
+    rows = pair.shape[0]
+    out[...] = jnp.swapaxes(
+        jnp.stack(
+            [
+                lax.dot_general(
+                    wt[...], pair[k], (((1,), (1,)), ((), ())),
+                    preferred_element_type=jnp.float32,
+                )
+                for k in range(rows)
+            ]
+        ),
+        0, 1,
+    )
+
+
+def bias(pair, wt, block=8):
+    R, C, width = pair.shape
+    heads = wt.shape[0]
+    return pl.pallas_call(
+        bias_kernel,
+        grid=(R // block,),
+        out_shape=jax.ShapeDtypeStruct((heads, R, C), jnp.float32),
+        in_specs=[
+            pl.BlockSpec((heads, width), lambda i: (0, 0)),
+            pl.BlockSpec((block, C, width), lambda i: (i, 0, 0)),
+        ],
+        out_specs=pl.BlockSpec((heads, block, C), lambda i: (0, i, 0)),
+    )(wt, pair)
+
+
+def pair_grad_kernel(wt, pair, ds, d_pair, wb):
+    rows = pair.shape[0]
+    by_row = jnp.swapaxes(ds[...].astype(jnp.float32), 0, 1).astype(jnp.bfloat16)
+
+    @pl.when(pl.program_id(0) == 0)
+    def _():
+        wb[...] = jnp.zeros_like(wb)
+
+    total = wb[...]
+    for k in range(rows):
+        one = by_row[k]
+        d_pair[k] = lax.dot_general(
+            one, wt[...], (((0,), (0,)), ((), ())), preferred_element_type=jnp.float32
+        ).astype(jnp.bfloat16)
+        total += jnp.dot(one, pair[k], preferred_element_type=jnp.float32)
+    wb[...] = total
+
+
+def pair_grad(pair, wt, ds, block=16):
+    R, C, width = pair.shape
+    heads = wt.shape[0]
+    return pl.pallas_call(
+        pair_grad_kernel,
+        grid=(R // block,),
+        out_shape=(
+            jax.ShapeDtypeStruct(pair.shape, jnp.bfloat16),
+            jax.ShapeDtypeStruct((heads, width), jnp.float32),
+        ),
+        in_specs=[
+            pl.BlockSpec((heads, width), lambda i: (0, 0)),
+            pl.BlockSpec((block, C, width), lambda i: (i, 0, 0)),
+            pl.BlockSpec((heads, block, C), lambda i: (0, i, 0)),
+        ],
+        out_specs=(
+            pl.BlockSpec((block, C, width), lambda i: (i, 0, 0)),
+            pl.BlockSpec((heads, width), lambda i: (0, 0)),
+        ),
+    )(wt, pair, ds)
+
+
 def on_device(nrow, ncol, pair, w_bias, queries, keys, values, d_out):
     R, C, width = pair.shape
     dcol, drow = queries.shape[1], keys.shape[1]
@@ -247,11 +318,11 @@
     out_heads = qd_all[:, :, dcol:].transpose(1, 0, 2).reshape(R, H, HD)
     key_heads = kv_all[:, :, :drow].transpose(1, 0, 2).reshape(C, H, HD)
     value_heads = kv_all[:, :, drow:].transpose(1, 0, 2).reshape(C, H, HD)
-    flat_pair = pair.reshape(R * C, width)
-    pair_bias = jnp.dot(flat_pair, w_bias, preferred_element_type=jnp.float32).reshape(R, C, H)
+    wt = w_bias.T
+    pair_bias = bias(pair, wt)
     scores = jnp.einsum(
         "ihd,jhd->hij", query_heads, key_heads, preferred_element_type=jnp.float32
-    ) * SCALE + pair_bias.transpose(2, 0, 1)
+    ) * SCALE + pair_bias
     grad_prob = jnp.einsum(
         "ihd,jhd->hij", out_heads, value_heads, preferred_element_type=jnp.float32
     )
@@ -260,18 +331,14 @@
     st = jnp.stack(
         [local_max, jnp.sum(exp_scores, axis=-1), jnp.sum(exp_scores * grad_prob, axis=-1)]
     )
-    st = st.reshape(3, ncol, H // ncol, R).transpose(1, 0, 2, 3)
+    count = H // ncol * R
+    lanes = 128 if count % 128 == 0 else R
+    st = st.reshape(3, ncol, count // lanes, lanes).transpose(1, 0, 2, 3)
     back = stats(ncol, st).transpose(1, 0, 2, 3).reshape(2, H, R)
     weights = exp_scores * back[0][..., None]
     grad_score = (weights * (grad_prob - back[1][..., None])).astype(jnp.bfloat16)
     weights_low = weights.astype(jnp.bfloat16)
-    score_flat = grad_score.transpose(1, 2, 0).reshape(R * C, H)
-    d_pair = (
-        jnp.dot(score_flat, w_bias.T, preferred_element_type=jnp.float32)
-        .astype(jnp.bfloat16)
-        .reshape(R, C, width)
-    )
-    weight_term = jnp.dot(score_flat.T, flat_pair, preferred_element_type=jnp.float32)
+    d_pair, weight_term = pair_grad(pair, wt, grad_score)
     query_term = jnp.einsum(
         "hij,jhd->ihd", grad_score, key_heads, preferred_element_type=jnp.float32
     ) * SCALE
@@ -282,12 +349,14 @@
         "hij,ihd->jhd", weights_low, out_heads, preferred_element_type=jnp.float32
     )
     dq = query_term.astype(jnp.bfloat16).reshape(R, ncol, dcol).transpose(1, 0, 2)
+    if R * dcol % 2048 == 0:
+        dq = dq.reshape(ncol, R * dcol // 128, 128)
     dk = key_term.astype(jnp.bfloat16).reshape(C, nrow, drow).transpose(1, 0, 2)
     dv = value_term.astype(jnp.bfloat16).reshape(C, nrow, drow).transpose(1, 0, 2)
     wb = weight_term.reshape(ncol, H // ncol, nrow, width // nrow).transpose(2, 0, 1, 3)
     wb, q_grad, kv_grad = reduce_all(nrow, ncol, wb, dq, jnp.concatenate([dk, dv], axis=2))
     d_wbias = wb.transpose(0, 3, 1, 2).reshape(width, H)
-    return d_pair, d_wbias, q_grad, kv_grad[:, :drow], kv_grad[:, drow:]
+    return d_pair, d_wbias, q_grad.reshape(R, dcol), kv_grad[:, :drow], kv_grad[:, drow:]
 
 
 def solution(mesh):

time: 251 us -> 189 us (0.75)
  local copies, waits for them, and re-layouts: 68.3 us -> 16.8 us
  Pallas kernels: 83.5 us -> 117 us
  matrix products: 66.8 us -> 37.4 us
  other arithmetic: 29.7 us -> 15.4 us
    pallas_call x0 -> x2, Pallas kernels: none -> 44.3 us  [the longest x1 22.4 us: pair_grad(): pl.pallas_call(pair_grad_kernel, grid=(R // block,), out_shape=(jax.Shape...]
    dot_general x3 -> x0, local copies, waits for them, and re-layouts: 41.6 us -> none  [the longest x2 29.6 us: on_device(): jnp.dot(score_flat.T, flat_pair, preferred_element_type=jnp.float32)]
    dot_general x3 -> x0, matrix products: 35 us -> none  [the longest x1 12.2 us: on_device(): jnp.dot(score_flat.T, flat_pair, preferred_element_type=jnp.float32)]
    convert_element_type x2 -> x1, other arithmetic: 24.7 us -> 10.5 us  [on_device(): (weights * (grad_prob - back[1][..., None])).astype(jnp.bfloat16)]
    pallas_call x1, Pallas kernels: 26.2 us -> 19.4 us  [stats(): pl.pallas_call(functools.partial(stats_kernel, ncol), out_shape=jax.Shape...]
    convert_element_type x1 -> x0, local copies, waits for them, and re-layouts: 6.75 us -> none  [on_device(): (weights * (grad_prob - back[1][..., None])).astype(jnp.bfloat16)]
    dot_general x1, matrix products: 7.58 us -> 13.6 us  [on_device(): jnp.einsum('ihd,jhd->hij', out_heads, value_heads, preferred_element_type...]
    reshape x1 -> x4, local copies, waits for them, and re-layouts: 9.2 us -> 5.12 us  [the longest x1 1.77 us: on_device(): dq = dq.reshape(ncol, R * dcol // 128, 128)]
where the time goes in v2:
time: 189 us; the launch traced here: 187 us
  Pallas kernels  117 us (62%)
  matrix products  37.4 us (20%)
  local copies, waits for them, and re-layouts  16.8 us (9%)
  other arithmetic  15.4 us (8%)
    pallas_call x1, Pallas kernels, gather(): pl.pallas_call(functools.partial(gather_kernel, nrow, ncol), out_shape=(j...  26.8 us
    pallas_call x1, Pallas kernels, reduce_all(): pl.pallas_call(functools.partial(reduce_kernel, nrow, ncol), out_shape=(j...  26.6 us
    pallas_call x1, Pallas kernels, pair_grad(): pl.pallas_call(pair_grad_kernel, grid=(R // block,), out_shape=(jax.Shape...  22.4 us
    pallas_call x1, Pallas kernels, bias(): pl.pallas_call(bias_kernel, grid=(R // block,), out_shape=jax.ShapeDtypeS...  21.9 us
    pallas_call x1, Pallas kernels, stats(): pl.pallas_call(functools.partial(stats_kernel, ncol), out_shape=jax.Shape...  19.4 us
    dot_general x1, matrix products, on_device(): jnp.einsum('ihd,jhd->hij', out_heads, value_heads, preferred_element_type...  13.6 us
    convert_element_type x1, other arithmetic, on_device(): (weights * (grad_prob - back[1][..., None])).astype(jnp.bfloat16)  10.5 us
    dot_general x1, matrix products, on_device(): jnp.einsum('ihd,jhd->hij', query_heads, key_heads, preferred_element_type...  9.25 us

profile of v2, /device:TPU:0, one launch (start us, length us, event | category | flops | bytes accessed | tf_op | source)
XLA Modules:
  0.0 187.4 jit_solution(6476698581459507507)
XLA Ops:
  0.6 1.7 pad_maximum_fusion.1.qd
  2.3 1.6 pad_maximum_fusion.2.kv
  3.9 26.8 %shard_map.101 = (bf16[8,192,384]{2,1,0:T(8,128)(2,1)}, bf16[4,96,768]{2,1,0:T(8,128)(2,1)}) custom-call(bf16[192,384]{1,0:T(8,128)(2,1)} %pad_maximum_fusion.1.qd, bf16[96,768]{1,0:T(8,128)(2,1)} %pad_maximum_fusion.2.kv), custom_call_target="tpu_custom_call" | custom-call | tf_op jit(solution)/shard_map/pallas_call | solution.py:77
  30.7 1.8 slice_bitcast_fusion.1
  32.8 1.1 slice_bitcast_fusion.3
  34.7 21.9 %shard_map.102 = f32[96,192,96]{2,1,0:T(8,128)} custom-call(bf16[96,512]{1,0:T(8,128)(2,1)} %bitcast.74, bf16[192,96,512]{2,1,0:T(8,128)(2,1)} %pair.3), custom_call_target="tpu_custom_call" | custom-call | tf_op jit(solution)/shard_map/pallas_call | solution.py:257
  56.6 9.3 %fusion.8 = (f32[96,192]{1,0:T(8,128)S(1)}, f32[96,192,96]{2,1,0:T(8,128)}) fusion(f32[96,192,96]{2,1,0:T(8,128)} %shard_map.102, bf16[192,96,16]{0,2,1:T(8,128)(2,1)S(1)} %bitcast.55, bf16[96,96,16]{0,2,1:T(8,128)(2,1)S(1)} %bitcast.59), kind=kOutput, calls=%fused_computation.25 | convolution fusion | flops 61913088 | bytes 15114240 | tf_op jit(solution)/shard_map/ihd,jhd->hij/dot_general | solution.py:323
  66.0 13.6 %fusion = (f32[96,192]{1,0:T(8,128)S(1)}, f32[96,192]{1,0:T(8,128)S(1)}, f32[96,192,96]{2,1,0:T(8,128)}) fusion(f32[96,192,96]{2,1,0:T(8,128)} %get-tuple-element.30, f32[96,192]{1,0:T(8,128)S(1)} %get-tuple-element.29, bf16[192,96,16]{0,2,1:T(8,128)(2,1)S(1)} %bitcast.57, bf16[96,96,16]{0,2,1:T(8,128)(2,1)S(1)} %bitcast.64), kind=kOutput, calls=%fused_computation.5 | convolution fusion | flops 63664128 | bytes 15261696 | tf_op jit(solution)/shard_map/ihd,jhd->hij/dot_general | solution.py:326
  79.7 0.7 maximum_bitcast_fusion.st
  80.5 19.4 %shard_map.103 = f32[8,2,18,128]{3,2,1,0:T(8,128)} custom-call(f32[8,3,18,128]{3,2,1,0:T(8,128)} %maximum_bitcast_fusion.st), custom_call_target="tpu_custom_call" | custom-call | tf_op jit(solution)/shard_map/pallas_call | solution.py:137
  99.8 1.0 fusion.6
  100.9 8.4 %fusion.4 = bf16[96,16,96]{2,1,0:T(8,128)(2,1)S(1)} fusion(bf16[192,96,16]{0,2,1:T(8,128)(2,1)S(1)} %bitcast.58, f32[96,192,96]{2,1,0:T(8,128)} %get-tuple-element.30, f32[96,192]{1,0:T(8,128)S(1)} %mul.39, f32[96,192]{1,0:T(8,128)S(1)} %get-tuple-element.29), kind=kOutput, calls=%fused_computation.11 | convolution fusion | flops 62078976 | bytes 8110080 | tf_op jit(solution)/shard_map/hij,ihd->jhd/dot_general | solution.py:348
  109.6 10.5 %multiply_convert_fusion.ds = bf16[96,192,96]{2,1,0:T(8,128)(2,1)S(1)} fusion(f32[96,192,96]{2,1,0:T(8,128)} %get-tuple-element.31, f32[96,192,96]{2,1,0:T(8,128)} %get-tuple-element.30, f32[96,192]{1,0:T(8,128)S(1)} %sub.20, f32[96,192]{1,0:T(8,128)S(1)} %mul.39, f32[96,192]{1,0:T(8,128)S(1)} %get-tuple-element.29), kind=kLoop, calls=%fused_computation | loop fusion | flops 8847360 | bytes 17915904 | tf_op jit(solution)/shard_map/convert_element_type | solution.py:339
  120.1 2.1 %copy-done = bf16[96,192,96]{2,1,0:T(8,128)(2,1)} copy-done((bf16[96,192,96]{2,1,0:T(8,128)(2,1)}, bf16[96,192,96]{2,1,0:T(8,128)(2,1)S(1)}, u32[]{:S(2)}) %copy-start) | copy-done | bytes 3538968
  122.2 1.4 fusion.5
  123.8 0.9 pad_maximum_fusion.dkv
  124.7 4.9 %multiply_convert_fusion.3 = bf16[96,16,192]{2,1,0:T(8,128)(2,1)S(1)} fusion(bf16[96,96,16]{0,2,1:T(8,128)(2,1)S(1)} %bitcast.60, bf16[96,192,96]{2,1,0:T(8,128)(2,1)} %copy-done), kind=kOutput, calls=%fused_computation.9 | convolution fusion | flops 57212928 | bytes 4423680 | tf_op jit(solution)/shard_map/hij,jhd->ihd/dot_general | solution.py:342
  129.9 1.8 reshape.64.dq
  131.7 22.4 %shard_map.104 = (bf16[192,96,512]{2,1,0:T(8,128)(2,1)}, f32[96,512]{1,0:T(8,128)}) custom-call(bf16[96,512]{1,0:T(8,128)(2,1)} %bitcast.75, bf16[192,96,512]{2,1,0:T(8,128)(2,1)} %pair.3, bf16[96,192,96]{2,1,0:T(8,128)(2,1)} %copy-done), custom_call_target="tpu_custom_call" | custom-call | tf_op jit(solution)/shard_map/pallas_call | solution.py:290
  154.1 1.0 reshape.62
  155.8 26.6 %shard_map.105 = (f32[4,8,12,128]{3,2,1,0:T(8,128)}, bf16[288,128]{1,0:T(8,128)(2,1)}, bf16[96,768]{1,0:T(8,128)(2,1)}) custom-call(f32[4,8,12,128]{3,2,1,0:T(8,128)} %bitcast.68, bf16[8,288,128]{2,1,0:T(8,128)(2,1)} %reshape.64.dq, bf16[4,96,768]{2,1,0:T(8,128)(2,1)} %pad_maximum_fusion.dkv), custom_call_target="tpu_custom_call" | custom-call | tf_op jit(solution)/shard_map/pallas_call | solution.py:214
  182.4 1.1 copy.29
  184.2 1.6 reshape.68
  185.8 1.6 fusion.7
  (15 shorter events, 3.8 us)
Async XLA Ops:
  120.1 2.1 %copy-start = (bf16[96,192,96]{2,1,0:T(8,128)(2,1)}, bf16[96,192,96]{2,1,0:T(8,128)(2,1)S(1)}, u32[]{:S(2)}) copy-start(bf16[96,192,96]{2,1,0:T(8,128)(2,1)S(1)} %multiply_convert_fusion.ds) | copy-start | bytes 10616836

commit v3 on v2

--- a/solution.py
+++ b/solution.py
@@ -35,56 +35,107 @@
     pl.semaphore_wait(barrier, ncol + nrow - 2)
 
 
-def gather_kernel(nrow, ncol, qd, kv, qd_all, kv_all, qs, qr, fs, fr, ks, kr):
+def gather_kernel(
+    nrow, ncol, wt, pair, qd, kv, out, qd_all, kv_all, qs, qr, fs, fr, ks, kr, own
+):
     row, col = lax.axis_index("row"), lax.axis_index("col")
     inner = 2 if ncol % 2 == 0 else 1
     outer = ncol // inner
     a, b = col // inner, lax.rem(col, inner)
-    greet(nrow, ncol, row, col)
-    sends = []
+    flip = a * inner + inner - 1 - b
+    step, last = pl.program_id(0), pl.num_programs(0) - 1
+    steps = out.shape[1]
+
+    def sends():
+        copies = []
+        for k in range(1, outer):
+            to = lax.rem(a + k, outer) * inner + b
+            copies.append(remote(qd, qd_all.at[col], qs.at[k], qr.at[k], row, to))
+        if inner == 2:
+            copies.append(remote(qd, qd_all.at[col], fs.at[0], fr.at[0], row, flip))
+        for k in range(1, nrow):
+            to = lax.rem(row + k, nrow)
+            copies.append(remote(kv, kv_all.at[row], ks.at[k], kr.at[k], to, col))
+        copies.append(pltpu.make_async_copy(qd, qd_all.at[col], own.at[0]))
+        copies.append(pltpu.make_async_copy(kv, kv_all.at[row], own.at[1]))
+        return copies
+
+    def relay(k):
+        src = lax.rem(a + outer - k, outer) * inner + b
+        return remote(qd_all.at[src], qd_all.at[src], fs.at[k], fr.at[k], row, flip)
+
+    @pl.when(step == 0)
+    def _():
+        greet(nrow, ncol, row, col)
+        for copy in sends():
+            copy.start()
+
+    out[...] = jnp.swapaxes(
+        jnp.stack(
+            [
+                lax.dot_general(
+                    wt[...], pair[k], (((1,), (1,)), ((), ())),
+                    preferred_element_type=jnp.float32,
+                )
+                for k in range(steps)
+            ]
+        ),
+        0, 1,
+    )
+
     for k in range(1, outer):
-        to = lax.rem(a + k, outer) * inner + b
-        sends.append(remote(qd, qd_all.at[col], qs.at[k], qr.at[k], row, to))
-    if inner == 2:
-        sends.append(remote(qd, qd_all.at[col], fs.at[0], fr.at[0], row, a * inner + 1 - b))
-    for k in range(1, nrow):
-        sends.append(remote(kv, kv_all.at[row], ks.at[k], kr.at[k], lax.rem(row + k, nrow), col))
-    for copy in sends:
-        copy.start()
-    qd_all[col] = qd[...]
-    kv_all[row] = kv[...]
-    for k in range(1, outer):
-        src = lax.rem(a + outer - k, outer) * inner + b
-        remote(qd, qd_all.at[src], qs.at[k], qr.at[k], row, col).wait_recv()
+
+        @pl.when(step == jnp.minimum(last, (last + 1) // 2 + 2 * (k - 1)))
+        def _():
+            src = lax.rem(a + outer - k, outer) * inner + b
+            remote(qd, qd_all.at[src], qs.at[k], qr.at[k], row, col).wait_recv()
+            if inner == 2:
+                relay(k).start()
+
+    @pl.when(step == last)
+    def _():
         if inner == 2:
-            copy = remote(
-                qd_all.at[src], qd_all.at[src], fs.at[k], fr.at[k], row, a * inner + 1 - b
-            )
-            copy.start()
-            sends.append(copy)
-    if inner == 2:
-        for k in range(outer):
-            src = lax.rem(a + outer - k, outer) * inner + 1 - b
-            remote(qd, qd_all.at[src], fs.at[k], fr.at[k], row, col).wait_recv()
-    for k in range(1, nrow):
-        src = lax.rem(row + nrow - k, nrow)
-        remote(kv, kv_all.at[src], ks.at[k], kr.at[k], row, col).wait_recv()
-    for copy in sends:
-        copy.wait_send()
-
-
-def gather(nrow, ncol, qd, kv):
+            for k in range(outer):
+                src = lax.rem(a + outer - k, outer) * inner + 1 - b
+                remote(qd, qd_all.at[src], fs.at[k], fr.at[k], row, col).wait_recv()
+        for k in range(1, nrow):
+            src = lax.rem(row + nrow - k, nrow)
+            remote(kv, kv_all.at[src], ks.at[k], kr.at[k], row, col).wait_recv()
+        copies = sends()
+        for copy in copies[:-2]:
+            copy.wait_send()
+        for copy in copies[-2:]:
+            copy.wait()
+        if inner == 2:
+            for k in range(1, outer):
+                relay(k).wait_send()
+
+
+def gather(nrow, ncol, pair, wt, qd, kv, block=8):
+    R, C, width = pair.shape
+    heads = wt.shape[0]
     return pl.pallas_call(
         functools.partial(gather_kernel, nrow, ncol),
+        grid=(R // block,),
         out_shape=(
+            jax.ShapeDtypeStruct((heads, R, C), jnp.float32),
             jax.ShapeDtypeStruct((ncol,) + qd.shape, qd.dtype),
             jax.ShapeDtypeStruct((nrow,) + kv.shape, kv.dtype),
         ),
-        in_specs=[pl.BlockSpec(memory_space=VMEM)] * 2,
-        out_specs=[pl.BlockSpec(memory_space=VMEM)] * 2,
-        scratch_shapes=[DMA((ncol,))] * 4 + [DMA((nrow,))] * 2,
+        in_specs=[
+            pl.BlockSpec((heads, width), lambda i: (0, 0)),
+            pl.BlockSpec((block, C, width), lambda i: (i, 0, 0)),
+            pl.BlockSpec(memory_space=pl.ANY),
+            pl.BlockSpec(memory_space=pl.ANY),
+        ],
+        out_specs=(
+            pl.BlockSpec((heads, block, C), lambda i: (0, i, 0)),
+            pl.BlockSpec(memory_space=pl.ANY),
+            pl.BlockSpec(memory_space=pl.ANY),
+        ),
+        scratch_shapes=[DMA((ncol,))] * 4 + [DMA((nrow,))] * 2 + [DMA((2,))],
         compiler_params=pltpu.CompilerParams(collective_id=0, has_side_effects=True),
-    )(qd, kv)
+    )(wt, pair, qd, kv)
 
 
 def stats_kernel(ncol, st, out, got, back, s1, r1, s2, r2):
@@ -149,8 +200,9 @@
 
 
 def reduce_kernel(
-    nrow, ncol, wb, dq, dkv, wb_out, q_out, kv_out,
-    w1, w1sum, w2, w2sum, qgot, kgot, ws1, wr1, ws2, wr2, ws3, wr3, ws4, wr4, qs, qr, ks, kr,
+    nrow, ncol, wb, dq, dkv, wb_out, q_out, k_out, v_out,
+    w1, w1sum, w2, w2sum, near, merged, far, kgot,
+    ws1, wr1, ws2, wr2, ws3, wr3, ws4, wr4, ns, nr, qs, qr, ks, kr,
 ):
     row, col = lax.axis_index("row"), lax.axis_index("col")
     greet(nrow, ncol, row, col)
@@ -163,9 +215,15 @@
     for k in range(1, nrow):
         to = lax.rem(row + k, nrow)
         go(remote(wb.at[to], w1.at[k], ws1.at[k], wr1.at[k], to, col))
-    for k in range(1, ncol):
-        to = lax.rem(col + k, ncol)
-        go(remote(dq.at[to], qgot.at[k], qs.at[k], qr.at[k], row, to))
+    inner = 2 if ncol % 2 == 0 else 1
+    outer = ncol // inner
+    a, b = col // inner, lax.rem(col, inner)
+    flip = a * inner + inner - 1 - b
+    order = list(range(1, outer)) + [0]
+    if inner == 2:
+        for k in order:
+            to = lax.rem(a + k, outer) * inner + 1 - b
+            go(remote(dq.at[to], near.at[k], ns.at[k], nr.at[k], row, flip))
     for k in range(1, nrow):
         to = lax.rem(row + k, nrow)
         go(remote(dkv.at[to], kgot.at[k], ks.at[k], kr.at[k], to, col))
@@ -174,9 +232,21 @@
         remote(wb.at[0], w1.at[k], ws1.at[k], wr1.at[k], row, col).wait_recv()
         total += w1[k]
     w1sum[...] = total
+
+    def pair_sum(k):
+        value = dq[lax.rem(a + k, outer) * inner + b].astype(jnp.float32)
+        if inner == 2:
+            remote(dq.at[0], near.at[k], ns.at[k], nr.at[k], row, col).wait_recv()
+            value += near[k].astype(jnp.float32)
+        return value
+
     for k in range(1, ncol):
         to = lax.rem(col + k, ncol)
         go(remote(w1sum.at[to], w2.at[k], ws2.at[k], wr2.at[k], row, to))
+    for k in range(1, outer):
+        merged[k] = pair_sum(k).astype(merged.dtype)
+        to = lax.rem(a + k, outer) * inner + b
+        go(remote(merged.at[k], far.at[k], qs.at[k], qr.at[k], row, to))
     part = w1sum[col]
     for k in range(1, ncol):
         remote(w1sum.at[0], w2.at[k], ws2.at[k], wr2.at[k], row, col).wait_recv()
@@ -196,11 +266,13 @@
     for k in range(1, nrow):
         remote(dkv.at[0], kgot.at[k], ks.at[k], kr.at[k], row, col).wait_recv()
         grad += kgot[k].astype(jnp.float32)
-    kv_out[...] = grad.astype(kv_out.dtype)
-    grad = dq[col].astype(jnp.float32)
-    for k in range(1, ncol):
-        remote(dq.at[0], qgot.at[k], qs.at[k], qr.at[k], row, col).wait_recv()
-        grad += qgot[k].astype(jnp.float32)
+    half = k_out.shape[1]
+    k_out[...] = grad[:, :half].astype(k_out.dtype)
+    v_out[...] = grad[:, half:].astype(v_out.dtype)
+    grad = pair_sum(0)
+    for k in range(1, outer):
+        remote(merged.at[k], far.at[k], qs.at[k], qr.at[k], row, col).wait_recv()
+        grad += far[k].astype(jnp.float32)
     q_out[...] = grad.astype(q_out.dtype)
     for k in range(1, nrow):
         src = lax.rem(row + nrow - k, nrow)
@@ -216,54 +288,26 @@
         out_shape=(
             jax.ShapeDtypeStruct(wb.shape, jnp.float32),
             jax.ShapeDtypeStruct(dq.shape[1:], jnp.bfloat16),
-            jax.ShapeDtypeStruct(dkv.shape[1:], jnp.bfloat16),
+            jax.ShapeDtypeStruct((dkv.shape[1], dkv.shape[2] // 2), jnp.bfloat16),
+            jax.ShapeDtypeStruct((dkv.shape[1], dkv.shape[2] // 2), jnp.bfloat16),
         ),
         in_specs=[pl.BlockSpec(memory_space=VMEM)] * 3,
-        out_specs=[pl.BlockSpec(memory_space=VMEM)] * 3,
+        out_specs=[pl.BlockSpec(memory_space=VMEM)] * 4,
         scratch_shapes=[
             VMEM(wb.shape, jnp.float32),
             VMEM((ncol,) + chunk, jnp.float32),
             VMEM((ncol,) + chunk, jnp.float32),
             VMEM(chunk, jnp.float32),
             VMEM(dq.shape, dq.dtype),
+            VMEM(dq.shape, dq.dtype),
+            VMEM(dq.shape, dq.dtype),
             VMEM(dkv.shape, dkv.dtype),
             DMA((nrow,)), DMA((nrow,)), DMA((ncol,)), DMA((ncol,)),
             DMA((ncol,)), DMA((ncol,)), DMA((nrow,)), DMA((nrow,)),
-            DMA((ncol,)), DMA((ncol,)), DMA((nrow,)), DMA((nrow,)),
+            DMA((ncol,)), DMA((ncol,)), DMA((ncol,)), DMA((ncol,)), DMA((nrow,)), DMA((nrow,)),
         ],
         compiler_params=pltpu.CompilerParams(collective_id=2, has_side_effects=True),
     )(wb, dq, dkv)
-
-
-def bias_kernel(wt, pair, out):
-    rows = pair.shape[0]
-    out[...] = jnp.swapaxes(
-        jnp.stack(
-            [
-                lax.dot_general(
-                    wt[...], pair[k], (((1,), (1,)), ((), ())),
-                    preferred_element_type=jnp.float32,
-                )
-                for k in range(rows)
-            ]
-        ),
-        0, 1,
-    )
-
-
-def bias(pair, wt, block=8):
-    R, C, width = pair.shape
-    heads = wt.shape[0]
-    return pl.pallas_call(
-        bias_kernel,
-        grid=(R // block,),
-        out_shape=jax.ShapeDtypeStruct((heads, R, C), jnp.float32),
-        in_specs=[
-            pl.BlockSpec((heads, width), lambda i: (0, 0)),
-            pl.BlockSpec((block, C, width), lambda i: (i, 0, 0)),
-        ],
-        out_specs=pl.BlockSpec((heads, block, C), lambda i: (0, i, 0)),
-    )(wt, pair)
 
 
 def pair_grad_kernel(wt, pair, ds, d_pair, wb):
@@ -309,8 +353,9 @@
 def on_device(nrow, ncol, pair, w_bias, queries, keys, values, d_out):
     R, C, width = pair.shape
     dcol, drow = queries.shape[1], keys.shape[1]
-    qd_all, kv_all = gather(
-        nrow, ncol,
+    wt = w_bias.T
+    pair_bias, qd_all, kv_all = gather(
+        nrow, ncol, pair, wt,
         jnp.concatenate([queries, d_out], axis=1),
         jnp.concatenate([keys, values], axis=1),
     )
@@ -318,8 +363,6 @@
     out_heads = qd_all[:, :, dcol:].transpose(1, 0, 2).reshape(R, H, HD)
     key_heads = kv_all[:, :, :drow].transpose(1, 0, 2).reshape(C, H, HD)
     value_heads = kv_all[:, :, drow:].transpose(1, 0, 2).reshape(C, H, HD)
-    wt = w_bias.T
-    pair_bias = bias(pair, wt)
     scores = jnp.einsum(
         "ihd,jhd->hij", query_heads, key_heads, preferred_element_type=jnp.float32
     ) * SCALE + pair_bias
@@ -354,9 +397,9 @@
     dk = key_term.astype(jnp.bfloat16).reshape(C, nrow, drow).transpose(1, 0, 2)
     dv = value_term.astype(jnp.bfloat16).reshape(C, nrow, drow).transpose(1, 0, 2)
     wb = weight_term.reshape(ncol, H // ncol, nrow, width // nrow).transpose(2, 0, 1, 3)
-    wb, q_grad, kv_grad = reduce_all(nrow, ncol, wb, dq, jnp.concatenate([dk, dv], axis=2))
+    wb, q_grad, k_grad, v_grad = reduce_all(nrow, ncol, wb, dq, jnp.concatenate([dk, dv], axis=2))
     d_wbias = wb.transpose(0, 3, 1, 2).reshape(width, H)
-    return d_pair, d_wbias, q_grad.reshape(R, dcol), kv_grad[:, :drow], kv_grad[:, drow:]
+    return d_pair, d_wbias, q_grad.reshape(R, dcol), k_grad, v_grad
 
 
 def solution(mesh):

time: 189 us -> 166 us (0.88)
  Pallas kernels: 117 us -> 92.5 us
    pallas_call x2 -> x1, Pallas kernels: 48.6 us -> 30.2 us  [gather(): pl.pallas_call(functools.partial(gather_kernel, nrow, ncol), grid=(R // b...]
    pallas_call x1, Pallas kernels: 26.6 us -> 23.5 us  [reduce_all(): pl.pallas_call(functools.partial(reduce_kernel, nrow, ncol), out_shape=(j...]
    unnamed x3 -> x5, local copies, waits for them, and re-layouts: 2.8 us -> 5.85 us
    pallas_call x1, Pallas kernels: 19.4 us -> 16.4 us  [stats(): pl.pallas_call(functools.partial(stats_kernel, ncol), out_shape=jax.Shape...]
where the time goes in v3:
time: 166 us; the launch traced here: 164 us
  Pallas kernels  92.5 us (56%)
  matrix products  37.4 us (23%)
  local copies, waits for them, and re-layouts  18.3 us (11%)
  other arithmetic  15.4 us (9%)
    pallas_call x1, Pallas kernels, gather(): pl.pallas_call(functools.partial(gather_kernel, nrow, ncol), grid=(R // b...  30.2 us
    pallas_call x1, Pallas kernels, reduce_all(): pl.pallas_call(functools.partial(reduce_kernel, nrow, ncol), out_shape=(j...  23.5 us
    pallas_call x1, Pallas kernels, pair_grad(): pl.pallas_call(pair_grad_kernel, grid=(R // block,), out_shape=(jax.Shape...  22.4 us
    pallas_call x1, Pallas kernels, stats(): pl.pallas_call(functools.partial(stats_kernel, ncol), out_shape=jax.Shape...  16.4 us
    dot_general x1, matrix products, on_device(): jnp.einsum('ihd,jhd->hij', out_heads, value_heads, preferred_element_type...  13.6 us
    convert_element_type x1, other arithmetic, on_device(): (weights * (grad_prob - back[1][..., None])).astype(jnp.bfloat16)  10.5 us
    dot_general x1, matrix products, on_device(): jnp.einsum('ihd,jhd->hij', query_heads, key_heads, preferred_element_type...  9.26 us
    dot_general x1, matrix products, on_device(): jnp.einsum('hij,ihd->jhd', weights_low, out_heads, preferred_element_type...  8.39 us

profile of v3, /device:TPU:0, one launch (start us, length us, event | category | flops | bytes accessed | tf_op | source)
XLA Modules:
  0.0 164.3 jit_solution(8436447034636911668)
XLA Ops:
  0.6 1.7 %pad_maximum_fusion.1.qd = bf16[192,384]{1,0:T(8,128)(2,1)} fusion(bf16[192,192]{1,0:T(8,128)(2,1)} %param.11, bf16[192,192]{1,0:T(8,128)(2,1)} %param.8), kind=kLoop, calls=%fused_computation.21 | loop fusion | flops 294912 | bytes 294912 | tf_op jit(solution)/shard_map/concatenate | solution.py:359
  2.3 1.6 pad_maximum_fusion.2.kv
  3.9 30.2 %shard_map.101 = (f32[96,192,96]{2,1,0:T(8,128)}, bf16[8,192,384]{2,1,0:T(8,128)(2,1)}, bf16[4,96,768]{2,1,0:T(8,128)(2,1)}) custom-call(bf16[96,512]{1,0:T(8,128)(2,1)} %bitcast.71, bf16[192,96,512]{2,1,0:T(8,128)(2,1)} %pair.3, bf16[192,384]{1,0:T(8,128)(2,1)} %pad_maximum_fusion.1.qd, bf16[96,768]{1,0:T(8,128)(2,1)} %pad_maximum_fusion.2.kv), custom_call_target="tpu_custom_call" | custom-call | tf_op jit(solution)/shard_map/pallas_call | solution.py:117
  34.1 1.8 %slice_bitcast_fusion.1 = (bf16[192,8,192]{2,0,1:T(8,128)(2,1)S(1)}, bf16[192,8,192]{2,0,1:T(8,128)(2,1)S(1)}) fusion(bf16[8,192,384]{2,1,0:T(8,128)(2,1)} %get-tuple-element.14), kind=kLoop, calls=%fused_computation.14 | loop fusion | bytes 2359296 | tf_op jit(solution)/shard_map/transpose | solution.py:362
  36.2 1.1 slice_bitcast_fusion.3
  37.6 9.3 %fusion.7 = (f32[96,192]{1,0:T(8,128)S(1)}, f32[96,192,96]{2,1,0:T(8,128)}) fusion(f32[96,192,96]{2,1,0:T(8,128)} %get-tuple-element.16, bf16[192,96,16]{0,2,1:T(8,128)(2,1)S(1)} %bitcast.55, bf16[96,96,16]{0,2,1:T(8,128)(2,1)S(1)} %bitcast.59), kind=kOutput, calls=%fused_computation.24 | convolution fusion | flops 61913088 | bytes 15114240 | tf_op jit(solution)/shard_map/ihd,jhd->hij/dot_general | solution.py:366
  47.5 13.6 %fusion = (f32[96,192]{1,0:T(8,128)S(1)}, f32[96,192]{1,0:T(8,128)S(1)}, f32[96,192,96]{2,1,0:T(8,128)}) fusion(f32[96,192,96]{2,1,0:T(8,128)} %get-tuple-element.32, f32[96,192]{1,0:T(8,128)S(1)} %get-tuple-element.31, bf16[192,96,16]{0,2,1:T(8,128)(2,1)S(1)} %bitcast.57, bf16[96,96,16]{0,2,1:T(8,128)(2,1)S(1)} %bitcast.64), kind=kOutput, calls=%fused_computation.5 | convolution fusion | flops 63664128 | bytes 15261696 | tf_op jit(solution)/shard_map/ihd,jhd->hij/dot_general | solution.py:369
  61.3 0.7 maximum_bitcast_fusion.st
  62.0 16.4 %shard_map.102 = f32[8,2,18,128]{3,2,1,0:T(8,128)} custom-call(f32[8,3,18,128]{3,2,1,0:T(8,128)} %maximum_bitcast_fusion.st), custom_call_target="tpu_custom_call" | custom-call | tf_op jit(solution)/shard_map/pallas_call | solution.py:188
  78.4 1.0 fusion.6
  79.5 8.4 %fusion.4 = bf16[96,16,96]{2,1,0:T(8,128)(2,1)S(1)} fusion(bf16[192,96,16]{0,2,1:T(8,128)(2,1)S(1)} %bitcast.58, f32[96,192,96]{2,1,0:T(8,128)} %get-tuple-element.32, f32[96,192]{1,0:T(8,128)S(1)} %mul.39, f32[96,192]{1,0:T(8,128)S(1)} %get-tuple-element.31), kind=kOutput, calls=%fused_computation.11 | convolution fusion | flops 62078976 | bytes 8110080 | tf_op jit(solution)/shard_map/hij,ihd->jhd/dot_general | solution.py:391
  88.1 10.5 %multiply_convert_fusion.ds = bf16[96,192,96]{2,1,0:T(8,128)(2,1)S(1)} fusion(f32[96,192,96]{2,1,0:T(8,128)} %get-tuple-element.33, f32[96,192,96]{2,1,0:T(8,128)} %get-tuple-element.32, f32[96,192]{1,0:T(8,128)S(1)} %sub.20, f32[96,192]{1,0:T(8,128)S(1)} %mul.39, f32[96,192]{1,0:T(8,128)S(1)} %get-tuple-element.31), kind=kLoop, calls=%fused_computation | loop fusion | flops 8847360 | bytes 17915904 | tf_op jit(solution)/shard_map/convert_element_type | solution.py:382
  98.7 2.1 %copy-done = bf16[96,192,96]{2,1,0:T(8,128)(2,1)} copy-done((bf16[96,192,96]{2,1,0:T(8,128)(2,1)}, bf16[96,192,96]{2,1,0:T(8,128)(2,1)S(1)}, u32[]{:S(2)}) %copy-start) | copy-done | bytes 3538968
  100.8 1.4 fusion.5
  102.3 0.9 pad_maximum_fusion.dkv
  103.2 4.9 %multiply_convert_fusion.3 = bf16[96,16,192]{2,1,0:T(8,128)(2,1)S(1)} fusion(bf16[96,96,16]{0,2,1:T(8,128)(2,1)S(1)} %bitcast.60, bf16[96,192,96]{2,1,0:T(8,128)(2,1)} %copy-done), kind=kOutput, calls=%fused_computation.9 | convolution fusion | flops 57212928 | bytes 4423680 | tf_op jit(solution)/shard_map/hij,jhd->ihd/dot_general | solution.py:385
  108.5 1.8 %reshape.64.dq = bf16[8,288,128]{2,1,0:T(8,128)(2,1)} reshape(bf16[8,192,192]{2,1,0:T(8,128)(2,1)S(1)} %bitcast.61) | data formatting | bytes 1179648 | tf_op jit(solution)/shard_map/reshape | solution.py:396
  110.2 22.4 %shard_map.103 = (bf16[192,96,512]{2,1,0:T(8,128)(2,1)}, f32[96,512]{1,0:T(8,128)}) custom-call(bf16[96,512]{1,0:T(8,128)(2,1)} %bitcast.72, bf16[192,96,512]{2,1,0:T(8,128)(2,1)} %pair.3, bf16[96,192,96]{2,1,0:T(8,128)(2,1)} %copy-done), custom_call_target="tpu_custom_call" | custom-call | tf_op jit(solution)/shard_map/pallas_call | solution.py:334
  132.6 1.0 reshape.62
  134.3 23.5 %shard_map.104 = (f32[4,8,12,128]{3,2,1,0:T(8,128)}, bf16[288,128]{1,0:T(8,128)(2,1)}, bf16[96,384]{1,0:T(8,128)(2,1)}, bf16[96,384]{1,0:T(8,128)(2,1)}) custom-call(f32[4,8,12,128]{3,2,1,0:T(8,128)} %bitcast.68, bf16[8,288,128]{2,1,0:T(8,128)(2,1)} %reshape.64.dq, bf16[4,96,768]{2,1,0:T(8,128)(2,1)} %pad_maximum_fusion.dkv), custom_call_target="tpu_custom_call" | custom-call | tf_op jit(solution)/shard_map/pallas_call | solution.py:286
  157.9 1.1 copy.29
  159.7 1.6 %reshape.68 = bf16[192,192]{1,0:T(8,128)(2,1)} reshape(bf16[288,128]{1,0:T(8,128)(2,1)} %get-tuple-element.20) | data formatting | bytes 147456 | tf_op jit(solution)/shard_map/reshape | solution.py:402
  161.3 1.5 copy.39
  162.8 1.5 copy.40
  (15 shorter events, 3.8 us)
Async XLA Ops:
  98.6 2.1 %copy-start = (bf16[96,192,96]{2,1,0:T(8,128)(2,1)}, bf16[96,192,96]{2,1,0:T(8,128)(2,1)S(1)}, u32[]{:S(2)}) copy-start(bf16[96,192,96]{2,1,0:T(8,128)(2,1)S(1)} %multiply_convert_fusion.ds) | copy-start | bytes 10616836

commit v4 on v3

--- a/solution.py
+++ b/solution.py
@@ -36,7 +36,8 @@
 
 
 def gather_kernel(
-    nrow, ncol, wt, pair, qd, kv, out, qd_all, kv_all, qs, qr, fs, fr, ks, kr, own
+    nrow, ncol, wt, pair, q, k_in, v, d, out, qd_all, kv_all,
+    qd, kv, qs, qr, fs, fr, ks, kr, own,
 ):
     row, col = lax.axis_index("row"), lax.axis_index("col")
     inner = 2 if ncol % 2 == 0 else 1
@@ -66,6 +67,8 @@
 
     @pl.when(step == 0)
     def _():
+        qd[...] = jnp.concatenate([q[...], d[...]], axis=1)
+        kv[...] = jnp.concatenate([k_in[...], v[...]], axis=1)
         greet(nrow, ncol, row, col)
         for copy in sends():
             copy.start()
@@ -111,8 +114,10 @@
                 relay(k).wait_send()
 
 
-def gather(nrow, ncol, pair, wt, qd, kv, block=8):
+def gather(nrow, ncol, pair, wt, q, k, v, d, block=8):
     R, C, width = pair.shape
+    qd = jax.ShapeDtypeStruct((R, 2 * q.shape[1]), q.dtype)
+    kv = jax.ShapeDtypeStruct((C, 2 * k.shape[1]), k.dtype)
     heads = wt.shape[0]
     return pl.pallas_call(
         functools.partial(gather_kernel, nrow, ncol),
@@ -125,17 +130,17 @@
         in_specs=[
             pl.BlockSpec((heads, width), lambda i: (0, 0)),
             pl.BlockSpec((block, C, width), lambda i: (i, 0, 0)),
-            pl.BlockSpec(memory_space=pl.ANY),
-            pl.BlockSpec(memory_space=pl.ANY),
-        ],
+        ]
+        + [pl.BlockSpec(memory_space=VMEM)] * 4,
         out_specs=(
             pl.BlockSpec((heads, block, C), lambda i: (0, i, 0)),
             pl.BlockSpec(memory_space=pl.ANY),
             pl.BlockSpec(memory_space=pl.ANY),
         ),
-        scratch_shapes=[DMA((ncol,))] * 4 + [DMA((nrow,))] * 2 + [DMA((2,))],
+        scratch_shapes=[VMEM(qd.shape, qd.dtype), VMEM(kv.shape, kv.dtype)]
+        + [DMA((ncol,))] * 4 + [DMA((nrow,))] * 2 + [DMA((2,))],
         compiler_params=pltpu.CompilerParams(collective_id=0, has_side_effects=True),
-    )(wt, pair, qd, kv)
+    )(wt, pair, q, k, v, d)
 
 
 def stats_kernel(ncol, st, out, got, back, s1, r1, s2, r2):
@@ -312,20 +317,23 @@
 
 def pair_grad_kernel(wt, pair, ds, d_pair, wb):
     rows = pair.shape[0]
-    by_row = jnp.swapaxes(ds[...].astype(jnp.float32), 0, 1).astype(jnp.bfloat16)
+    cols, width = pair.shape[1:]
+    by_row = jnp.swapaxes(ds[...].astype(jnp.float32), 0, 1)
+    flat = jnp.swapaxes(by_row, 1, 2).astype(jnp.bfloat16).reshape(rows * cols, -1)
 
     @pl.when(pl.program_id(0) == 0)
     def _():
         wb[...] = jnp.zeros_like(wb)
 
-    total = wb[...]
-    for k in range(rows):
-        one = by_row[k]
-        d_pair[k] = lax.dot_general(
-            one, wt[...], (((0,), (0,)), ((), ())), preferred_element_type=jnp.float32
-        ).astype(jnp.bfloat16)
-        total += jnp.dot(one, pair[k], preferred_element_type=jnp.float32)
-    wb[...] = total
+    d_pair[...] = (
+        jnp.dot(flat, wt[...], preferred_element_type=jnp.float32)
+        .astype(jnp.bfloat16)
+        .reshape(rows, cols, width)
+    )
+    wb[...] += lax.dot_general(
+        flat, pair[...].reshape(rows * cols, width), (((0,), (0,)), ((), ())),
+        preferred_element_type=jnp.float32,
+    )
 
 
 def pair_grad(pair, wt, ds, block=16):
@@ -356,8 +364,7 @@
     wt = w_bias.T
     pair_bias, qd_all, kv_all = gather(
         nrow, ncol, pair, wt,
-        jnp.concatenate([queries, d_out], axis=1),
-        jnp.concatenate([keys, values], axis=1),
+        queries, keys, values, d_out,
     )
     query_heads = qd_all[:, :, :dcol].transpose(1, 0, 2).reshape(R, H, HD)
     out_heads = qd_all[:, :, dcol:].transpose(1, 0, 2).reshape(R, H, HD)

time: 166 us -> 160 us (0.964)
  other arithmetic: 15.4 us -> 12.1 us
  Pallas kernels: 92.5 us -> 90 us
    concatenate x2 -> x0, other arithmetic: 3.29 us -> none  [the longest x1 1.7 us: on_device(): jnp.concatenate([queries, d_out], axis=1)]
    pallas_call x1, Pallas kernels: 22.4 us -> 20 us  [pair_grad(): pl.pallas_call(pair_grad_kernel, grid=(R // block,), out_shape=(jax.Shape...]
where the time goes in v4:
time: 160 us; the launch traced here: 159 us
  Pallas kernels  90 us (56%)
  matrix products  37.4 us (23%)
  local copies, waits for them, and re-layouts  18.3 us (11%)
  other arithmetic  12.1 us (8%)
    pallas_call x1, Pallas kernels, gather(): pl.pallas_call(functools.partial(gather_kernel, nrow, ncol), grid=(R // b...  30.4 us
    pallas_call x1, Pallas kernels, reduce_all(): pl.pallas_call(functools.partial(reduce_kernel, nrow, ncol), out_shape=(j...  22.9 us
    pallas_call x1, Pallas kernels, pair_grad(): pl.pallas_call(pair_grad_kernel, grid=(R // block,), out_shape=(jax.Shape...  20 us
    pallas_call x1, Pallas kernels, stats(): pl.pallas_call(functools.partial(stats_kernel, ncol), out_shape=jax.Shape...  16.7 us
    dot_general x1, matrix products, on_device(): jnp.einsum('ihd,jhd->hij', out_heads, value_heads, preferred_element_type...  13.6 us
    convert_element_type x1, other arithmetic, on_device(): (weights * (grad_prob - back[1][..., None])).astype(jnp.bfloat16)  10.5 us
    dot_general x1, matrix products, on_device(): jnp.einsum('ihd,jhd->hij', query_heads, key_heads, preferred_element_type...  9.26 us
    dot_general x1, matrix products, on_device(): jnp.einsum('hij,ihd->jhd', weights_low, out_heads, preferred_element_type...  8.39 us

profile of v4, /device:TPU:0, one launch (start us, length us, event | category | flops | bytes accessed | tf_op | source)
XLA Modules:
  0.0 158.6 jit_solution(3602308892660159538)
XLA Ops:
  0.6 30.4 %shard_map.101 = (f32[96,192,96]{2,1,0:T(8,128)}, bf16[8,192,384]{2,1,0:T(8,128)(2,1)}, bf16[4,96,768]{2,1,0:T(8,128)(2,1)}) custom-call(bf16[96,512]{1,0:T(8,128)(2,1)} %bitcast.71, bf16[192,96,512]{2,1,0:T(8,128)(2,1)} %pair.3, bf16[192,192]{1,0:T(8,128)(2,1)} %q.1, bf16[96,384]{1,0:T(8,128)(2,1)} %k_in.1, bf16[96,384]{1,0:T(8,128)(2,1)} %v.1, ...), custom_call_target="tpu_custom_call" | custom-call | tf_op jit(solution)/shard_map/pallas_call | solution.py:122
  31.1 1.8 %slice_bitcast_fusion.1 = (bf16[192,8,192]{2,0,1:T(8,128)(2,1)S(1)}, bf16[192,8,192]{2,0,1:T(8,128)(2,1)S(1)}) fusion(bf16[8,192,384]{2,1,0:T(8,128)(2,1)} %get-tuple-element.14), kind=kLoop, calls=%fused_computation.14 | loop fusion | bytes 2359296 | tf_op jit(solution)/shard_map/transpose | solution.py:369
  33.2 1.1 slice_bitcast_fusion.3
  34.5 9.3 %fusion.7 = (f32[96,192]{1,0:T(8,128)S(1)}, f32[96,192,96]{2,1,0:T(8,128)}) fusion(f32[96,192,96]{2,1,0:T(8,128)} %get-tuple-element.16, bf16[192,96,16]{0,2,1:T(8,128)(2,1)S(1)} %bitcast.55, bf16[96,96,16]{0,2,1:T(8,128)(2,1)S(1)} %bitcast.59), kind=kOutput, calls=%fused_computation.22 | convolution fusion | flops 61913088 | bytes 15114240 | tf_op jit(solution)/shard_map/ihd,jhd->hij/dot_general | solution.py:373
  44.5 13.6 %fusion = (f32[96,192]{1,0:T(8,128)S(1)}, f32[96,192]{1,0:T(8,128)S(1)}, f32[96,192,96]{2,1,0:T(8,128)}) fusion(f32[96,192,96]{2,1,0:T(8,128)} %get-tuple-element.32, f32[96,192]{1,0:T(8,128)S(1)} %get-tuple-element.31, bf16[192,96,16]{0,2,1:T(8,128)(2,1)S(1)} %bitcast.57, bf16[96,96,16]{0,2,1:T(8,128)(2,1)S(1)} %bitcast.64), kind=kOutput, calls=%fused_computation.5 | convolution fusion | flops 63664128 | bytes 15261696 | tf_op jit(solution)/shard_map/ihd,jhd->hij/dot_general | solution.py:376
  58.2 0.7 maximum_bitcast_fusion.st
  59.0 16.7 %shard_map.102 = f32[8,2,18,128]{3,2,1,0:T(8,128)} custom-call(f32[8,3,18,128]{3,2,1,0:T(8,128)} %maximum_bitcast_fusion.st), custom_call_target="tpu_custom_call" | custom-call | tf_op jit(solution)/shard_map/pallas_call | solution.py:193
  75.7 1.0 fusion.6
  76.7 8.4 %fusion.4 = bf16[96,16,96]{2,1,0:T(8,128)(2,1)S(1)} fusion(bf16[192,96,16]{0,2,1:T(8,128)(2,1)S(1)} %bitcast.58, f32[96,192,96]{2,1,0:T(8,128)} %get-tuple-element.32, f32[96,192]{1,0:T(8,128)S(1)} %mul.39, f32[96,192]{1,0:T(8,128)S(1)} %get-tuple-element.31), kind=kOutput, calls=%fused_computation.11 | convolution fusion | flops 62078976 | bytes 8110080 | tf_op jit(solution)/shard_map/hij,ihd->jhd/dot_general | solution.py:398
  85.4 10.5 %multiply_convert_fusion.ds = bf16[96,192,96]{2,1,0:T(8,128)(2,1)S(1)} fusion(f32[96,192,96]{2,1,0:T(8,128)} %get-tuple-element.33, f32[96,192,96]{2,1,0:T(8,128)} %get-tuple-element.32, f32[96,192]{1,0:T(8,128)S(1)} %sub.20, f32[96,192]{1,0:T(8,128)S(1)} %mul.39, f32[96,192]{1,0:T(8,128)S(1)} %get-tuple-element.31), kind=kLoop, calls=%fused_computation | loop fusion | flops 8847360 | bytes 17915904 | tf_op jit(solution)/shard_map/convert_element_type | solution.py:389
  95.9 2.1 %copy-done = bf16[96,192,96]{2,1,0:T(8,128)(2,1)} copy-done((bf16[96,192,96]{2,1,0:T(8,128)(2,1)}, bf16[96,192,96]{2,1,0:T(8,128)(2,1)S(1)}, u32[]{:S(2)}) %copy-start) | copy-done | bytes 3538968
  98.0 1.4 fusion.5
  99.6 0.9 pad_maximum_fusion.dkv
  100.5 4.9 %multiply_convert_fusion.3 = bf16[96,16,192]{2,1,0:T(8,128)(2,1)S(1)} fusion(bf16[96,96,16]{0,2,1:T(8,128)(2,1)S(1)} %bitcast.60, bf16[96,192,96]{2,1,0:T(8,128)(2,1)} %copy-done), kind=kOutput, calls=%fused_computation.9 | convolution fusion | flops 57212928 | bytes 4423680 | tf_op jit(solution)/shard_map/hij,jhd->ihd/dot_general | solution.py:392
  105.7 1.8 %reshape.64.dq = bf16[8,288,128]{2,1,0:T(8,128)(2,1)} reshape(bf16[8,192,192]{2,1,0:T(8,128)(2,1)S(1)} %bitcast.61) | data formatting | bytes 1179648 | tf_op jit(solution)/shard_map/reshape | solution.py:403
  107.5 20.0 %shard_map.103 = (bf16[192,96,512]{2,1,0:T(8,128)(2,1)}, f32[96,512]{1,0:T(8,128)}) custom-call(bf16[96,512]{1,0:T(8,128)(2,1)} %bitcast.72, bf16[192,96,512]{2,1,0:T(8,128)(2,1)} %pair.3, bf16[96,192,96]{2,1,0:T(8,128)(2,1)} %copy-done), custom_call_target="tpu_custom_call" | custom-call | tf_op jit(solution)/shard_map/pallas_call | solution.py:342
  127.5 1.0 reshape.62
  128.5 0.7 copy.35
  129.2 22.9 %shard_map.104 = (f32[4,8,12,128]{3,2,1,0:T(8,128)}, bf16[288,128]{1,0:T(8,128)(2,1)}, bf16[96,384]{1,0:T(8,128)(2,1)}, bf16[96,384]{1,0:T(8,128)(2,1)}) custom-call(f32[4,8,12,128]{3,2,1,0:T(8,128)} %bitcast.68, bf16[8,288,128]{2,1,0:T(8,128)(2,1)} %reshape.64.dq, bf16[4,96,768]{2,1,0:T(8,128)(2,1)} %pad_maximum_fusion.dkv), custom_call_target="tpu_custom_call" | custom-call | tf_op jit(solution)/shard_map/pallas_call | solution.py:291
  152.2 1.1 copy.29
  153.2 0.7 copy.36
  153.9 1.6 %reshape.68 = bf16[192,192]{1,0:T(8,128)(2,1)} reshape(bf16[288,128]{1,0:T(8,128)(2,1)} %get-tuple-element.20) | data formatting | bytes 147456 | tf_op jit(solution)/shard_map/reshape | solution.py:409
  155.6 1.5 copy.39
  157.1 1.5 copy.40
  (13 shorter events, 2.4 us)
Async XLA Ops:
  95.9 2.1 %copy-start = (bf16[96,192,96]{2,1,0:T(8,128)(2,1)}, bf16[96,192,96]{2,1,0:T(8,128)(2,1)S(1)}, u32[]{:S(2)}) copy-start(bf16[96,192,96]{2,1,0:T(8,128)(2,1)S(1)} %multiply_convert_fusion.ds) | copy-start | bytes 10616836
